TPU v7x, 256 devices: a whole 4x4x8 slice. The times are simulated.
256 devices in a mesh: dp: 32 (over y, x, z_lo), cam: 8 (over z_hi, core).
Axes of the slice: x: 4, y: 4, z: 8 (z_hi: 4, z_lo: 2; z = z_hi * 2 + z_lo), core: 2. Of those that a mesh axis runs over, the one named last changes fastest.
Arguments:
- grad_out: bfloat16 [32768, 3072], P(('dp', 'cam')), may hold values from -6 to 6
- query_act: bfloat16 [32768, 2048], P(('dp', 'cam')), may hold values from -13 to 13
- key_act: bfloat16 [32768, 2048], P(('dp', 'cam')), may hold values from -13 to 13
- value_act: bfloat16 [32768, 2048], P(('dp', 'cam')), may hold values from -6 to 6
- out_proj: bfloat16 [3072, 2048], P('dp'), may hold values from -0.125 to 0.125
- view_counts: int32 [32, 4], P('dp'), may hold values from 1 to 12, 16 in all within a row
- view_slots: int32 [32, 16], P('dp'), may hold values from 0 to 15, each once within a row
Outputs:
- grad_query: bfloat16 [32768, 2048], P(('dp', 'cam'))
- grad_key: bfloat16 [32768, 2048], P(('dp', 'cam'))
- grad_value: bfloat16 [32768, 2048], P(('dp', 'cam'))
- grad_proj: float32 [3072, 2048], P('dp')
Inputs may be any that keep to these rules, and one draw needn't show every extreme that they name: `view_counts`: in each group the 4 counts sum to 16, and the largest is exactly 12. `view_slots`: each row is a permutation of the group's 16 slots.
All inputs are finite; a program needn't handle non-finite values.
Results may differ from a plain program's by a relative error of at most 0.0096.
Values may be sent and summed in bfloat16 or wider, within the bound.
A program may use at most 64 MiB of HBM per device.

v0:
```python
import math

import jax
import jax.numpy as jnp
from jax import lax
from jax.sharding import PartitionSpec as P

HEAD_DIM = 128
VIEW_TOK = 64


def token_objects(counts, slots, view_tokens):
    count_ends = jnp.cumsum(counts)
    view_order = jnp.arange(slots.shape[0], dtype=jnp.int32)
    view_object = jnp.sum((view_order[:, None] >= count_ends[None, :]).astype(jnp.int32), axis=1)
    placed = slots[:, None] == view_order[None, :]
    slot_object = jnp.sum(jnp.where(placed, view_object[:, None], 0), axis=0)
    return jnp.repeat(slot_object, view_tokens)


def head_attention(query_heads, key_heads, value_heads, grad_heads, same_object, head_dim):
    group_tokens, proj_width = query_heads.shape
    head_count = proj_width // head_dim
    score_scale = 1.0 / math.sqrt(head_dim)

    def one_head(head_index):
        first_col = head_index * head_dim
        query_one = lax.dynamic_slice_in_dim(query_heads, first_col, head_dim, 1)
        key_one = lax.dynamic_slice_in_dim(key_heads, first_col, head_dim, 1)
        value_one = lax.dynamic_slice_in_dim(value_heads, first_col, head_dim, 1)
        grad_one = lax.dynamic_slice_in_dim(grad_heads, first_col, head_dim, 1)
        scores = (
            lax.dot_general(
                query_one, key_one, (((1,), (1,)), ((), ())), preferred_element_type=jnp.float32
            )
            * score_scale
        )
        scores = jnp.where(same_object, scores, -jnp.inf)
        row_max = jnp.max(scores, axis=1, keepdims=True)
        exp_scores = jnp.exp(scores - row_max)
        probs = exp_scores / jnp.sum(exp_scores, axis=1, keepdims=True)
        probs_bf16 = probs.astype(jnp.bfloat16)
        attended_f32 = jnp.dot(probs_bf16, value_one, preferred_element_type=jnp.float32)
        row_delta = jnp.sum(grad_one.astype(jnp.float32) * attended_f32, axis=1)
        grad_probs = lax.dot_general(
            grad_one, value_one, (((1,), (1,)), ((), ())), preferred_element_type=jnp.float32
        )
        grad_scores = (probs * (grad_probs - row_delta[:, None])).astype(jnp.bfloat16)
        grad_query = jnp.dot(grad_scores, key_one, preferred_element_type=jnp.float32) * score_scale
        grad_key = (
            lax.dot_general(
                grad_scores, query_one, (((0,), (0,)), ((), ())), preferred_element_type=jnp.float32
            )
            * score_scale
        )
        grad_value = lax.dot_general(
            probs_bf16, grad_one, (((0,), (0,)), ((), ())), preferred_element_type=jnp.float32
        )
        return (
            attended_f32.astype(jnp.bfloat16),
            grad_query.astype(jnp.bfloat16),
            grad_key.astype(jnp.bfloat16),
            grad_value.astype(jnp.bfloat16),
        )

    stacked = lax.map(one_head, jnp.arange(head_count, dtype=jnp.int32))

    def flatten(per_head):
        return jnp.transpose(per_head, (1, 0, 2)).reshape(group_tokens, proj_width)

    return tuple((flatten(item) for item in stacked))


def local(grad_out, query_act, key_act, value_act, out_proj, view_counts, view_slots):
    objects = token_objects(view_counts[0], view_slots[0], VIEW_TOK)
    same_object = objects[:, None] == objects[None, :]
    whole_out = lax.all_gather(grad_out, "cam", axis=0, tiled=True)
    columns = grad_out
    grad_attn = jnp.dot(
        columns,
        lax.all_gather(out_proj, "dp", axis=0, tiled=True),
        preferred_element_type=jnp.float32,
    ).astype(jnp.bfloat16)
    query_heads, key_heads, value_heads, grad_heads = (
        lax.all_to_all(query_act, "cam", split_axis=1, concat_axis=0, tiled=True),
        lax.all_to_all(key_act, "cam", split_axis=1, concat_axis=0, tiled=True),
        lax.all_to_all(value_act, "cam", split_axis=1, concat_axis=0, tiled=True),
        lax.all_to_all(grad_attn, "cam", split_axis=1, concat_axis=0, tiled=True),
    )
    attended, grad_query, grad_key, grad_value = head_attention(
        query_heads, key_heads, value_heads, grad_heads, same_object, HEAD_DIM
    )
    columns = whole_out
    partial_rows = lax.psum_scatter(
        lax.dot_general(
            columns, attended, (((0,), (0,)), ((), ())), preferred_element_type=jnp.float32
        ),
        "dp",
        scatter_dimension=0,
        tiled=True,
    )
    grad_proj = lax.all_gather(partial_rows, "cam", axis=1, tiled=True)
    grad_query, grad_key, grad_value = (
        lax.all_to_all(grad_query, "cam", split_axis=0, concat_axis=1, tiled=True),
        lax.all_to_all(grad_key, "cam", split_axis=0, concat_axis=1, tiled=True),
        lax.all_to_all(grad_value, "cam", split_axis=0, concat_axis=1, tiled=True),
    )
    return (grad_query, grad_key, grad_value, grad_proj)


def solution(mesh):
    in_specs = (
        P(("dp", "cam"), None),
        P(("dp", "cam"), None),
        P(("dp", "cam"), None),
        P(("dp", "cam"), None),
        P("dp", None),
        P("dp", None),
        P("dp", None),
    )
    out_specs = (
        P(("dp", "cam"), None),
        P(("dp", "cam"), None),
        P(("dp", "cam"), None),
        P("dp", None),
    )
    return jax.shard_map(local, mesh=mesh, in_specs=in_specs, out_specs=out_specs, check_vma=False)
```

profile of v0, /device:TPU:1, one launch (start us, length us, event | category | flops | bytes accessed | tf_op | source)
XLA Modules:
  0.0 621.5 jit_solution(6285375771550483284)
XLA Ops:
  8.7 1.9 copy.106
  10.5 10.0 %all-to-all-start = ((bf16[128,8,256]{2,0,1:T(8,128)(2,1)}), bf16[128,8,256]{2,0,1:T(8,128)(2,1)S(1)}, u32[]{:S(2)}, u32[]{:S(2)}) async-start(bf16[128,8,256]{2,0,1:T(8,128)(2,1)} %bitcast.86), calls=%async_computation | async-start | bytes 1048576 | tf_op jit(solution)/shard_map/all_to_all | solution.py:85
  20.5 1.9 copy.105
  22.4 17.7 %all-to-all-done = bf16[128,8,256]{2,0,1:T(8,128)(2,1)S(1)} async-done(((bf16[128,8,256]{2,0,1:T(8,128)(2,1)}), bf16[128,8,256]{2,0,1:T(8,128)(2,1)S(1)}, u32[]{:S(2)}, u32[]{:S(2)}) %all-to-all-start) | async-done | bytes 524320 | tf_op jit(solution)/shard_map/all_to_all | solution.py:85
  40.1 5.0 all-to-all-start.1
  45.1 0.8 copy.104
  45.9 22.4 %all-to-all-done.1 = bf16[128,8,256]{2,0,1:T(8,128)(2,1)S(1)} async-done(((bf16[128,8,256]{2,0,1:T(8,128)(2,1)}), bf16[128,8,256]{2,0,1:T(8,128)(2,1)S(1)}, u32[]{:S(2)}, u32[]{:S(2)}) %all-to-all-start.1) | async-done | bytes 524320 | tf_op jit(solution)/shard_map/all_to_all | solution.py:86
  68.3 4.0 all-to-all-start.2
  72.3 250.5 %all-gather.3.cloned.1.call-done = bf16[3072,2048]{1,0:T(8,128)(2,1)} async-done(((bf16[96,2048]{1,0:T(8,128)(2,1)}), bf16[3072,2048]{1,0:T(8,128)(2,1)}) %all-gather.3.cloned.1.call-update) | async-done | bytes 12582928 | tf_op jit(solution)/shard_map/all_gather | solution.py:81
  322.8 6.4 %convolution_convert_fusion.1 = bf16[128,2048]{1,0:T(8,128)(2,1)S(1)} fusion(bf16[128,3072]{1,0:T(8,128)(2,1)S(1)} %copy-done.2, bf16[3072,2048]{1,0:T(8,128)(2,1)} %all-gather.3.cloned.1.call-done), kind=kOutput, calls=%fused_computation.37 | convolution fusion | flops 1610874880 | bytes 13893632 | tf_op jit(solution)/shard_map/dot_general | solution.py:79
  329.2 0.8 copy.103
  330.0 6.9 %all-to-all-start.3 = ((bf16[128,8,256]{2,0,1:T(8,128)(2,1)}), bf16[128,8,256]{2,0,1:T(8,128)(2,1)S(1)}, u32[]{:S(2)}, u32[]{:S(2)}) async-start(bf16[128,8,256]{2,0,1:T(8,128)(2,1)} %bitcast.83), calls=%async_computation.3 | async-start | bytes 1048576 | tf_op jit(solution)/shard_map/all_to_all | solution.py:88
  337.5 35.0 %all-to-all-done.3 = bf16[128,8,256]{2,0,1:T(8,128)(2,1)S(1)} async-done(((bf16[128,8,256]{2,0,1:T(8,128)(2,1)}), bf16[128,8,256]{2,0,1:T(8,128)(2,1)S(1)}, u32[]{:S(2)}, u32[]{:S(2)}) %all-to-all-start.3) | async-done | bytes 524320 | tf_op jit(solution)/shard_map/all_to_all | solution.py:88
  372.5 30.3 %while.17 = (s32[]{:T(128)}, bf16[2,1024,128]{1,2,0:T(8,128)(2,1)}, bf16[2,1024,128]{2,1,0:T(8,128)(2,1)S(1)}, bf16[2,1024,128]{2,1,0:T(8,128)(2,1)}, bf16[2,102...) while((s32[]{:T(128)}, bf16[2,1024,128]{1,2,0:T(8,128)(2,1)}, ...), condition=%wide.region_7.8_spmd.clone, body=%wide.region_3.7_spmd.clone.sunk | while | flops 1631712256 | bytes 87341000 | solution.py:66
  374.5 1.0 fusion.59
  375.5 1.4 fusion.60
  376.9 1.9 copy-done
  378.9 1.2 bitcast_dynamic-update-slice_fusion.2
  380.4 3.0 multiply_convert_fusion.2
  384.2 0.9 fusion.61
  385.9 0.9 fusion.63
  389.6 1.0 fusion.59
  390.6 1.4 fusion.60
  392.0 1.9 copy-done
  394.0 1.2 bitcast_dynamic-update-slice_fusion.2
  395.5 3.0 multiply_convert_fusion.2
  399.4 0.9 fusion.61
  401.1 0.8 fusion.63
  402.7 1.1 all-gather.5.cloned.1.call-done
  403.8 4.8 convolution_bitcast_fusion
  408.6 2.4 copy.89
  411.0 1.3 copy.78
  412.4 0.9 copy.79
  413.3 3.7 all-to-all-start.4
  417.3 0.9 copy.81
  418.2 18.1 %all-to-all-done.4 = bf16[8,128,256]{1,2,0:T(8,128)(2,1)S(1)} async-done(((bf16[8,128,256]{1,2,0:T(8,128)(2,1)}), bf16[8,128,256]{1,2,0:T(8,128)(2,1)S(1)}, u32[]{:S(2)}, u32[]{:S(2)}) %all-to-all-start.4) | async-done | bytes 524320 | tf_op jit(solution)/shard_map/all_to_all | solution.py:104
  436.3 4.9 all-to-all-start.5
  441.5 0.9 copy.83
  442.4 20.0 %all-to-all-done.5 = bf16[8,128,256]{1,2,0:T(8,128)(2,1)S(1)} async-done(((bf16[8,128,256]{1,2,0:T(8,128)(2,1)}), bf16[8,128,256]{1,2,0:T(8,128)(2,1)S(1)}, u32[]{:S(2)}, u32[]{:S(2)}) %all-to-all-start.5) | async-done | bytes 524320 | tf_op jit(solution)/shard_map/all_to_all | solution.py:105
  462.4 4.4 all-to-all-start.6
  466.7 1.0 copy.84
  467.7 1.0 copy.85
  468.7 20.9 %all-to-all-done.6 = bf16[8,128,256]{1,2,0:T(8,128)(2,1)S(1)} async-done(((bf16[8,128,256]{1,2,0:T(8,128)(2,1)}), bf16[8,128,256]{1,2,0:T(8,128)(2,1)S(1)}, u32[]{:S(2)}, u32[]{:S(2)}) %all-to-all-start.6) | async-done | bytes 524320 | tf_op jit(solution)/shard_map/all_to_all | solution.py:106
  489.6 1.0 copy.86
  490.6 81.5 %reduce-scatter.4.cloned.1.call-done = f32[96,256]{1,0:T(8,128)} async-done(((f32[3072,256]{1,0:T(8,128)}), f32[96,256]{1,0:T(8,128)}) %reduce-scatter.4.cloned.1.call-update) | async-done | bytes 98320
  572.2 1.0 copy.90
  573.1 40.6 %all_gather.11 = f32[96,2048]{0,1:T(8,128)S(1)} all-gather(f32[96,256]{0,1:T(8,128)S(1)} %copy.90), channel_id=1, replica_groups=mesh['dp'=32,'cam'=8] {'cam'}, dimensions={1}, use_global_device_ids=true | all-gather | bytes 884736 | tf_op jit(solution)/shard_map/all_gather | solution.py:102
  613.7 1.2 copy.87
  (78 shorter events, 10.9 us)
Async XLA Ops:
  7.2 315.7 %copy-start.2 = (bf16[128,3072]{1,0:T(8,128)(2,1)S(1)}, bf16[128,3072]{1,0:T(8,128)(2,1)}, u32[]{:S(2)}) copy-start(bf16[128,3072]{1,0:T(8,128)(2,1)} %param.9) | copy-start | bytes 2359300
  7.2 37.9 %copy-start.3 = (bf16[128,2048]{1,0:T(8,128)(2,1)S(1)}, bf16[128,2048]{1,0:T(8,128)(2,1)}, u32[]{:S(2)}) copy-start(bf16[128,2048]{1,0:T(8,128)(2,1)} %param.12) | copy-start | bytes 1572868
  7.2 315.6 %all-gather.3.cloned.1.call-start = ((), (), s32[]{:S(2)}) async-start(), calls=%async_computation.8 | async-start | bytes 12976128 | tf_op jit(solution)/shard_map/all_gather | solution.py:81
  7.9 395.9 %all-gather.5.cloned.1.call-start = ((), (), s32[]{:S(2)}) async-start(), calls=%async_computation.9 | async-start | bytes 7077888 | tf_op jit(solution)/shard_map/all_gather | solution.py:77
  10.5 29.5 %all-to-all-start = ((bf16[128,8,256]{2,0,1:T(8,128)(2,1)}), bf16[128,8,256]{2,0,1:T(8,128)(2,1)S(1)}, u32[]{:S(2)}, u32[]{:S(2)}) async-start(bf16[128,8,256]{2,0,1:T(8,128)(2,1)} %bitcast.86), calls=%async_computation | async-start | bytes 1048576 | tf_op jit(solution)/shard_map/all_to_all | solution.py:85
  40.1 28.2 %all-to-all-start.1 = ((bf16[128,8,256]{2,0,1:T(8,128)(2,1)}), bf16[128,8,256]{2,0,1:T(8,128)(2,1)S(1)}, u32[]{:S(2)}, u32[]{:S(2)}) async-start(bf16[128,8,256]{2,0,1:T(8,128)(2,1)} %bitcast.85), calls=%async_computation.1 | async-start | bytes 1048576 | tf_op jit(solution)/shard_map/all_to_all | solution.py:86
  68.3 261.7 %all-to-all-start.2 = ((bf16[128,8,256]{2,0,1:T(8,128)(2,1)}), bf16[128,8,256]{2,0,1:T(8,128)(2,1)S(1)}, u32[]{:S(2)}, u32[]{:S(2)}) async-start(bf16[128,8,256]{2,0,1:T(8,128)(2,1)} %bitcast.84), calls=%async_computation.2 | async-start | bytes 1048576 | tf_op jit(solution)/shard_map/all_to_all | solution.py:87
  72.3 264.6 %copy-start.13 = (s32[1,4]{1,0:T(1,128)S(1)}, s32[1,4]{1,0:T(1,128)}, u32[]{:S(2)}) copy-start(s32[1,4]{1,0:T(1,128)} %param.14) | copy-start | bytes 52
  72.3 264.9 %copy-start.14 = (s32[1,16]{1,0:T(1,128)S(1)}, s32[1,16]{1,0:T(1,128)}, u32[]{:S(2)}) copy-start(s32[1,16]{1,0:T(1,128)} %param.15) | copy-start | bytes 196
  330.0 42.4 %all-to-all-start.3 = ((bf16[128,8,256]{2,0,1:T(8,128)(2,1)}), bf16[128,8,256]{2,0,1:T(8,128)(2,1)S(1)}, u32[]{:S(2)}, u32[]{:S(2)}) async-start(bf16[128,8,256]{2,0,1:T(8,128)(2,1)} %bitcast.83), calls=%async_computation.3 | async-start | bytes 1048576 | tf_op jit(solution)/shard_map/all_to_all | solution.py:88
  336.9 235.2 %reduce-scatter.4.cloned.1.call-start = ((), (), s32[]{:S(2)}) async-start(), calls=%async_computation.10 | async-start | bytes 3244032
  372.5 3.0 copy-start.4
  376.9 1.9 copy-start
  380.3 3.1 copy-start.7
  380.4 3.9 copy-start.5
  383.4 2.4 copy-start.1
  383.4 2.5 copy-start.10
  384.2 0.9 copy-start.8
  386.8 0.8 copy-start.11
  387.6 3.0 copy-start.4
  392.0 1.9 copy-start
  395.4 3.2 copy-start.7
  395.5 3.9 copy-start.5
  398.5 2.4 copy-start.1
  398.5 2.5 copy-start.10
  399.4 0.9 copy-start.8
  401.9 0.8 copy-start.11
  402.7 1.1 copy-start.6
  410.9 6.1 copy-start.9
  411.0 30.2 %copy-start.12 = (bf16[2,1024,128]{2,1,0:T(8,128)(2,1)S(1)}, bf16[2,1024,128]{2,1,0:T(8,128)(2,1)}, u32[]{:S(2)}) copy-start(bf16[2,1024,128]{2,1,0:T(8,128)(2,1)} %get-tuple-element.66) | copy-start | bytes 1572868
  413.3 23.0 %all-to-all-start.4 = ((bf16[8,128,256]{1,2,0:T(8,128)(2,1)}), bf16[8,128,256]{1,2,0:T(8,128)(2,1)S(1)}, u32[]{:S(2)}, u32[]{:S(2)}) async-start(bf16[8,128,256]{1,2,0:T(8,128)(2,1)} %copy.79), calls=%async_computation.4 | async-start | bytes 1048576 | tf_op jit(solution)/shard_map/all_to_all | solution.py:104
  436.3 26.1 %all-to-all-start.5 = ((bf16[8,128,256]{1,2,0:T(8,128)(2,1)}), bf16[8,128,256]{1,2,0:T(8,128)(2,1)S(1)}, u32[]{:S(2)}, u32[]{:S(2)}) async-start(bf16[8,128,256]{1,2,0:T(8,128)(2,1)} %copy.81), calls=%async_computation.5 | async-start | bytes 1048576 | tf_op jit(solution)/shard_map/all_to_all | solution.py:105
  462.4 27.3 %all-to-all-start.6 = ((bf16[8,128,256]{1,2,0:T(8,128)(2,1)}), bf16[8,128,256]{1,2,0:T(8,128)(2,1)S(1)}, u32[]{:S(2)}, u32[]{:S(2)}) async-start(bf16[8,128,256]{1,2,0:T(8,128)(2,1)} %copy.83), calls=%async_computation.6 | async-start | bytes 1048576 | tf_op jit(solution)/shard_map/all_to_all | solution.py:106
Sparse Core Ops, SparseCore 0:
  9.8 312.9 all-gather.2
  324.6 79.1 all-gather.4
  411.1 161.0 reduce-scatter.3
where the time goes:
time: 622 us; the launch traced here: 621 us
  waiting for transfers between devices  469 us (75%)
  blocking collectives  40.6 us (7%)
  starting transfers between devices  38.9 us (6%)
  local copies, waits for them, and re-layouts  26.6 us (4%)
  matrix products  26.2 us (4%)
  between operations  13.9 us (2%)
    all_gather x1, waiting for transfers between devices, local(): lax.all_gather(out_proj, 'dp', axis=0, tiled=True)  250 us
    unnamed x4, waiting for transfers between devices  82.9 us
    all_gather x1, blocking collectives, local(): grad_proj = lax.all_gather(partial_rows, 'cam', axis=1, tiled=True)  40.6 us
    all_to_all x1, waiting for transfers between devices, local(): lax.all_to_all(grad_attn, 'cam', split_axis=1, concat_axis=0, tiled=True)  35 us
    all_to_all x1, waiting for transfers between devices, local(): lax.all_to_all(key_act, 'cam', split_axis=1, concat_axis=0, tiled=True)  22.4 us
    all_to_all x1, waiting for transfers between devices, local(): lax.all_to_all(grad_value, 'cam', split_axis=0, concat_axis=1, tiled=True)  20.9 us
    all_to_all x1, waiting for transfers between devices, local(): lax.all_to_all(grad_key, 'cam', split_axis=0, concat_axis=1, tiled=True)  20 us
    all_to_all x1, waiting for transfers between devices, local(): lax.all_to_all(grad_query, 'cam', split_axis=0, concat_axis=1, tiled=True)  18.1 us
  transfers between devices with their start and end apart: 10, of which 9 were waited for; matrix products, arithmetic and copies ran while one was open for 7% of the time, Pallas kernels for 0%

commit v1 on v0

--- a/solution.py
+++ b/solution.py
@@ -74,31 +74,29 @@
 def local(grad_out, query_act, key_act, value_act, out_proj, view_counts, view_slots):
     objects = token_objects(view_counts[0], view_slots[0], VIEW_TOK)
     same_object = objects[:, None] == objects[None, :]
+    cam = lax.axis_index("cam")
+    width = query_act.shape[1] // lax.axis_size("cam")
+    out_columns = lax.dynamic_slice_in_dim(out_proj, cam * width, width, 1)
+    out_columns = lax.all_gather(out_columns, "dp", axis=0, tiled=True)
     whole_out = lax.all_gather(grad_out, "cam", axis=0, tiled=True)
-    columns = grad_out
-    grad_attn = jnp.dot(
-        columns,
-        lax.all_gather(out_proj, "dp", axis=0, tiled=True),
-        preferred_element_type=jnp.float32,
-    ).astype(jnp.bfloat16)
-    query_heads, key_heads, value_heads, grad_heads = (
+    query_heads, key_heads, value_heads = (
         lax.all_to_all(query_act, "cam", split_axis=1, concat_axis=0, tiled=True),
         lax.all_to_all(key_act, "cam", split_axis=1, concat_axis=0, tiled=True),
         lax.all_to_all(value_act, "cam", split_axis=1, concat_axis=0, tiled=True),
-        lax.all_to_all(grad_attn, "cam", split_axis=1, concat_axis=0, tiled=True),
+    )
+    grad_heads = jnp.dot(whole_out, out_columns, preferred_element_type=jnp.float32).astype(
+        jnp.bfloat16
     )
     attended, grad_query, grad_key, grad_value = head_attention(
         query_heads, key_heads, value_heads, grad_heads, same_object, HEAD_DIM
     )
-    columns = whole_out
-    partial_rows = lax.psum_scatter(
-        lax.dot_general(
-            columns, attended, (((0,), (0,)), ((), ())), preferred_element_type=jnp.float32
-        ),
-        "dp",
-        scatter_dimension=0,
-        tiled=True,
-    )
+    partial = lax.dot_general(
+        whole_out, attended, (((0,), (0,)), ((), ())), preferred_element_type=jnp.float32
+    ).astype(jnp.bfloat16)
+    dp = lax.axis_size("dp")
+    rows = partial.shape[0] // dp
+    pieces = lax.all_to_all(partial, "dp", split_axis=0, concat_axis=0, tiled=True)
+    partial_rows = jnp.sum(pieces.reshape(dp, rows, width).astype(jnp.float32), axis=0)
     grad_proj = lax.all_gather(partial_rows, "cam", axis=1, tiled=True)
     grad_query, grad_key, grad_value = (
         lax.all_to_all(grad_query, "cam", split_axis=0, concat_axis=1, tiled=True),

time: 622 us -> 395 us (0.64)
  waiting for transfers between devices: 469 us -> 270 us
  blocking collectives: 40.6 us -> 21.2 us
  local copies, waits for them, and re-layouts: 26.6 us -> 19.1 us
    all_gather x1, waiting for transfers between devices: 250 us -> 92.7 us  [local(): out_columns = lax.all_gather(out_columns, 'dp', axis=0, tiled=True)]
    all_gather x1, waiting for transfers between devices: 1.09 us -> 88.8 us  [local(): whole_out = lax.all_gather(grad_out, 'cam', axis=0, tiled=True)]
    unnamed x4 -> x2, waiting for transfers between devices: 82.9 us -> 0.71 us
    all_gather x1, blocking collectives: 40.6 us -> 21.2 us  [local(): grad_proj = lax.all_gather(partial_rows, 'cam', axis=1, tiled=True)]
    all_to_all x1, waiting for transfers between devices: 35 us -> 16.8 us  [local(): lax.all_to_all(partial, 'dp', split_axis=0, concat_axis=0, tiled=True)]
    all_to_all x1, waiting for transfers between devices: 20.9 us -> 8.98 us  [local(): lax.all_to_all(grad_value, 'cam', split_axis=0, concat_axis=1, tiled=True)]
    all_to_all x1, waiting for transfers between devices: 20 us -> 12.3 us  [local(): lax.all_to_all(grad_key, 'cam', split_axis=0, concat_axis=1, tiled=True)]
  transfers between devices with their start and end apart: 10 -> 9, of which waited for: 9 -> 8; matrix products, arithmetic and copies ran while one was open for 7% -> 6% of each run, Pallas kernels for 0% -> 0%
where the time goes in v1:
time: 395 us; the launch traced here: 394 us
  waiting for transfers between devices  270 us (68%)
  starting transfers between devices  42.5 us (11%)
  blocking collectives  21.2 us (5%)
  matrix products  20.1 us (5%)
  local copies, waits for them, and re-layouts  19.1 us (5%)
  between operations  14.2 us (4%)
  other arithmetic  5.62 us (1%)
    all_gather x1, waiting for transfers between devices, local(): out_columns = lax.all_gather(out_columns, 'dp', axis=0, tiled=True)  92.7 us
    all_gather x1, waiting for transfers between devices, local(): whole_out = lax.all_gather(grad_out, 'cam', axis=0, tiled=True)  88.8 us
    all_gather x1, blocking collectives, local(): grad_proj = lax.all_gather(partial_rows, 'cam', axis=1, tiled=True)  21.2 us
    all_to_all x1, waiting for transfers between devices, local(): lax.all_to_all(key_act, 'cam', split_axis=1, concat_axis=0, tiled=True)  19.7 us
    all_to_all x1, waiting for transfers between devices, local(): lax.all_to_all(partial, 'dp', split_axis=0, concat_axis=0, tiled=True)  16.8 us
    all_to_all x1, waiting for transfers between devices, local(): lax.all_to_all(query_act, 'cam', split_axis=1, concat_axis=0, tiled=True)  15 us
    all_to_all x1, waiting for transfers between devices, local(): lax.all_to_all(grad_query, 'cam', split_axis=0, concat_axis=1, tiled=True)  14.5 us
    all_to_all x1, waiting for transfers between devices, local(): lax.all_to_all(grad_key, 'cam', split_axis=0, concat_axis=1, tiled=True)  12.3 us
  transfers between devices with their start and end apart: 9, of which 8 were waited for; matrix products, arithmetic and copies ran while one was open for 6% of the time, Pallas kernels for 0%

profile of v1, /device:TPU:1, one launch (start us, length us, event | category | flops | bytes accessed | tf_op | source)
XLA Modules:
  0.0 393.6 jit_solution(17446073319802578734)
XLA Ops:
  7.3 0.9 copy-done
  9.6 1.9 copy.92
  11.4 10.0 %all-to-all-start = ((bf16[128,8,256]{2,0,1:T(8,128)(2,1)}), bf16[128,8,256]{2,0,1:T(8,128)(2,1)S(1)}, u32[]{:S(2)}, u32[]{:S(2)}) async-start(bf16[128,8,256]{2,0,1:T(8,128)(2,1)} %bitcast.79), calls=%async_computation | async-start | bytes 1048576 | tf_op jit(solution)/shard_map/all_to_all | solution.py:83
  21.4 1.9 copy.91
  23.3 15.0 %all-to-all-done = bf16[128,8,256]{2,0,1:T(8,128)(2,1)S(1)} async-done(((bf16[128,8,256]{2,0,1:T(8,128)(2,1)}), bf16[128,8,256]{2,0,1:T(8,128)(2,1)S(1)}, u32[]{:S(2)}, u32[]{:S(2)}) %all-to-all-start) | async-done | bytes 524320 | tf_op jit(solution)/shard_map/all_to_all | solution.py:83
  38.3 5.9 %all-to-all-start.1 = ((bf16[128,8,256]{2,0,1:T(8,128)(2,1)}), bf16[128,8,256]{2,0,1:T(8,128)(2,1)S(1)}, u32[]{:S(2)}, u32[]{:S(2)}) async-start(bf16[128,8,256]{2,0,1:T(8,128)(2,1)} %bitcast.78), calls=%async_computation.1 | async-start | bytes 1048576 | tf_op jit(solution)/shard_map/all_to_all | solution.py:84
  44.2 0.8 copy.90
  45.0 19.7 %all-to-all-done.1 = bf16[128,8,256]{2,0,1:T(8,128)(2,1)S(1)} async-done(((bf16[128,8,256]{2,0,1:T(8,128)(2,1)}), bf16[128,8,256]{2,0,1:T(8,128)(2,1)S(1)}, u32[]{:S(2)}, u32[]{:S(2)}) %all-to-all-start.1) | async-done | bytes 524320 | tf_op jit(solution)/shard_map/all_to_all | solution.py:84
  64.7 3.9 all-to-all-start.2
  69.1 92.7 %all-gather.3.cloned.1.call-done = bf16[3072,256]{1,0:T(8,128)(2,1)} async-done(((bf16[96,256]{1,0:T(8,128)(2,1)}), bf16[3072,256]{1,0:T(8,128)(2,1)}) %all-gather.3.cloned.1.call-update) | async-done | bytes 1572880 | tf_op jit(solution)/shard_map/all_gather | solution.py:80
  161.9 88.8 %all-gather.5.cloned.1.call-done = bf16[1024,3072]{1,0:T(8,128)(2,1)} async-done(((bf16[128,3072]{1,0:T(8,128)(2,1)}), bf16[1024,3072]{1,0:T(8,128)(2,1)}) %all-gather.5.cloned.1.call-update) | async-done | bytes 6291472 | tf_op jit(solution)/shard_map/all_gather | solution.py:81
  250.7 5.1 %fusion.32 = bf16[1024,256]{0,1:T(8,128)(2,1)S(1)} fusion(bf16[3072,256]{1,0:T(8,128)(2,1)} %all-gather.3.cloned.1.call-done, bf16[1024,3072]{1,0:T(8,128)(2,1)} %all-gather.5.cloned.1.call-done), kind=kOutput, calls=%fused_computation.42 | convolution fusion | flops 1610874880 | bytes 8388608 | tf_op jit(solution)/shard_map/dot_general | solution.py:87
  255.8 19.5 %while.17 = (s32[]{:T(128)}, bf16[2,1024,128]{1,2,0:T(8,128)(2,1)}, bf16[2,1024,128]{2,1,0:T(8,128)(2,1)S(1)}, bf16[2,1024,128]{2,1,0:T(8,128)(2,1)S(1)}, bf16[2...) while((s32[]{:T(128)}, bf16[2,1024,128]{1,2,0:T(8,128)(2,1)}, ...), condition=%wide.region_7.8_spmd.clone, body=%wide.region_3.7_spmd.clone.sunk | while | flops 1631712256 | bytes 44350236 | solution.py:66
  257.1 0.7 fusion.61
  257.8 1.0 fusion.62
  258.9 1.4 fusion.63
  260.8 0.8 copy-done.3
  261.7 0.7 multiply_convert_fusion.2
  262.4 0.8 fusion.65
  263.2 0.9 fusion.64
  264.1 1.4 fusion.66
  266.8 0.7 fusion.61
  267.5 1.0 fusion.62
  268.6 1.4 fusion.63
  270.5 0.8 copy-done.3
  271.4 0.7 multiply_convert_fusion.2
  272.1 0.8 fusion.65
  273.0 0.9 fusion.64
  273.8 1.4 fusion.66
  275.6 0.9 copy.71
  276.5 4.1 %all-to-all-start.3 = ((bf16[8,128,256]{1,2,0:T(8,128)(2,1)}), bf16[8,128,256]{1,2,0:T(8,128)(2,1)S(1)}, u32[]{:S(2)}, u32[]{:S(2)}) async-start(bf16[8,128,256]{1,2,0:T(8,128)(2,1)} %copy.71), calls=%async_computation.3 | async-start | bytes 1048576 | tf_op jit(solution)/shard_map/all_to_all | solution.py:102
  280.9 0.9 copy.73
  281.8 14.5 %all-to-all-done.3 = bf16[8,128,256]{1,2,0:T(8,128)(2,1)S(1)} async-done(((bf16[8,128,256]{1,2,0:T(8,128)(2,1)}), bf16[8,128,256]{1,2,0:T(8,128)(2,1)S(1)}, u32[]{:S(2)}, u32[]{:S(2)}) %all-to-all-start.3) | async-done | bytes 524320 | tf_op jit(solution)/shard_map/all_to_all | solution.py:102
  296.2 4.5 %all-to-all-start.4 = ((bf16[8,128,256]{1,2,0:T(8,128)(2,1)}), bf16[8,128,256]{1,2,0:T(8,128)(2,1)S(1)}, u32[]{:S(2)}, u32[]{:S(2)}) async-start(bf16[8,128,256]{1,2,0:T(8,128)(2,1)} %copy.73), calls=%async_computation.4 | async-start | bytes 1048576 | tf_op jit(solution)/shard_map/all_to_all | solution.py:103
  300.7 1.2 copy.74
  302.1 0.9 copy.75
  302.9 12.3 %all-to-all-done.4 = bf16[8,128,256]{1,2,0:T(8,128)(2,1)S(1)} async-done(((bf16[8,128,256]{1,2,0:T(8,128)(2,1)}), bf16[8,128,256]{1,2,0:T(8,128)(2,1)S(1)}, u32[]{:S(2)}, u32[]{:S(2)}) %all-to-all-start.4) | async-done | bytes 524320 | tf_op jit(solution)/shard_map/all_to_all | solution.py:103
  315.2 7.3 %all-to-all-start.5 = ((bf16[8,128,256]{1,2,0:T(8,128)(2,1)}), bf16[8,128,256]{1,2,0:T(8,128)(2,1)S(1)}, u32[]{:S(2)}, u32[]{:S(2)}) async-start(bf16[8,128,256]{1,2,0:T(8,128)(2,1)} %copy.75), calls=%async_computation.5 | async-start | bytes 1048576 | tf_op jit(solution)/shard_map/all_to_all | solution.py:104
  322.5 4.8 %fusion.31 = bf16[3072,256]{0,1:T(8,128)(2,1)S(1)} fusion(bf16[1024,256]{0,1:T(8,128)(2,1)} %bitcast.111, bf16[1024,3072]{1,0:T(8,128)(2,1)} %all-gather.5.cloned.1.call-done), kind=kOutput, calls=%fused_computation.39 | convolution fusion | flops 1611399168 | bytes 8388608 | tf_op jit(solution)/shard_map/dot_general | solution.py:93
  327.2 1.6 copy.76
  328.8 9.0 %all-to-all-done.5 = bf16[8,128,256]{1,2,0:T(8,128)(2,1)S(1)} async-done(((bf16[8,128,256]{1,2,0:T(8,128)(2,1)}), bf16[8,128,256]{1,2,0:T(8,128)(2,1)S(1)}, u32[]{:S(2)}, u32[]{:S(2)}) %all-to-all-start.5) | async-done | bytes 524320 | tf_op jit(solution)/shard_map/all_to_all | solution.py:104
  337.8 6.8 %all-to-all-start.6 = ((bf16[32,96,256]{2,1,0:T(8,128)(2,1)}), bf16[32,96,256]{2,1,0:T(8,128)(2,1)S(1)}, u32[]{:S(2)}, u32[]{:S(2)}) async-start(bf16[32,96,256]{2,1,0:T(8,128)(2,1)} %bitcast.22), calls=%async_computation.6 | async-start | bytes 3145728 | tf_op jit(solution)/shard_map/all_to_all | solution.py:98
  344.6 1.0 copy.77
  345.7 1.0 copy.78
  346.7 1.0 copy.79
  347.7 16.8 %all-to-all-done.6 = bf16[32,96,256]{2,1,0:T(8,128)(2,1)S(1)} async-done(((bf16[32,96,256]{2,1,0:T(8,128)(2,1)}), bf16[32,96,256]{2,1,0:T(8,128)(2,1)S(1)}, u32[]{:S(2)}, u32[]{:S(2)}) %all-to-all-start.6) | async-done | bytes 1572896 | tf_op jit(solution)/shard_map/all_to_all | solution.py:98
  364.7 21.2 %all_gather.11 = f32[96,2048]{1,0:T(8,128)S(1)} all-gather(f32[96,256]{1,0:T(8,128)S(1)} %convert_reduce_fusion), channel_id=1, replica_groups=mesh['dp'=32,'cam'=8] {'cam'}, dimensions={1}, use_global_device_ids=true | all-gather | bytes 884736 | tf_op jit(solution)/shard_map/all_gather | solution.py:100
  385.9 0.9 copy.113
  (41 shorter events, 5.3 us)
Async XLA Ops:
  7.2 1.0 copy-start
  7.2 37.0 %copy-start.1 = (bf16[128,2048]{1,0:T(8,128)(2,1)S(1)}, bf16[128,2048]{1,0:T(8,128)(2,1)}, u32[]{:S(2)}) copy-start(bf16[128,2048]{1,0:T(8,128)(2,1)} %param.12) | copy-start | bytes 1572868
  7.2 61.4 %copy-start.4 = (s32[1,4]{1,0:T(1,128)S(1)}, s32[1,4]{1,0:T(1,128)}, u32[]{:S(2)}) copy-start(s32[1,4]{1,0:T(1,128)} %param.14) | copy-start | bytes 52
  7.2 61.7 %copy-start.5 = (s32[1,16]{1,0:T(1,128)S(1)}, s32[1,16]{1,0:T(1,128)}, u32[]{:S(2)}) copy-start(s32[1,16]{1,0:T(1,128)} %param.15) | copy-start | bytes 196
  7.2 154.6 %all-gather.3.cloned.1.call-start = ((), (), s32[]{:S(2)}) async-start(), calls=%async_computation.7 | async-start | bytes 1622016 | tf_op jit(solution)/shard_map/all_gather | solution.py:80
  8.8 241.9 %all-gather.5.cloned.1.call-start = ((), (), s32[]{:S(2)}) async-start(), calls=%async_computation.8 | async-start | bytes 7077888 | tf_op jit(solution)/shard_map/all_gather | solution.py:81
  11.4 26.8 %all-to-all-start = ((bf16[128,8,256]{2,0,1:T(8,128)(2,1)}), bf16[128,8,256]{2,0,1:T(8,128)(2,1)S(1)}, u32[]{:S(2)}, u32[]{:S(2)}) async-start(bf16[128,8,256]{2,0,1:T(8,128)(2,1)} %bitcast.79), calls=%async_computation | async-start | bytes 1048576 | tf_op jit(solution)/shard_map/all_to_all | solution.py:83
  38.3 26.5 %all-to-all-start.1 = ((bf16[128,8,256]{2,0,1:T(8,128)(2,1)}), bf16[128,8,256]{2,0,1:T(8,128)(2,1)S(1)}, u32[]{:S(2)}, u32[]{:S(2)}) async-start(bf16[128,8,256]{2,0,1:T(8,128)(2,1)} %bitcast.78), calls=%async_computation.1 | async-start | bytes 1048576 | tf_op jit(solution)/shard_map/all_to_all | solution.py:84
  64.7 191.1 %all-to-all-start.2 = ((bf16[128,8,256]{2,0,1:T(8,128)(2,1)}), bf16[128,8,256]{2,0,1:T(8,128)(2,1)S(1)}, u32[]{:S(2)}, u32[]{:S(2)}) async-start(bf16[128,8,256]{2,0,1:T(8,128)(2,1)} %bitcast.77), calls=%async_computation.2 | async-start | bytes 1048576 | tf_op jit(solution)/shard_map/all_to_all | solution.py:85
  258.8 1.4 copy-start.2
  260.8 0.8 copy-start.3
  268.6 1.4 copy-start.2
  270.5 0.8 copy-start.3
  276.5 19.7 %all-to-all-start.3 = ((bf16[8,128,256]{1,2,0:T(8,128)(2,1)}), bf16[8,128,256]{1,2,0:T(8,128)(2,1)S(1)}, u32[]{:S(2)}, u32[]{:S(2)}) async-start(bf16[8,128,256]{1,2,0:T(8,128)(2,1)} %copy.71), calls=%async_computation.3 | async-start | bytes 1048576 | tf_op jit(solution)/shard_map/all_to_all | solution.py:102
  296.2 19.0 %all-to-all-start.4 = ((bf16[8,128,256]{1,2,0:T(8,128)(2,1)}), bf16[8,128,256]{1,2,0:T(8,128)(2,1)S(1)}, u32[]{:S(2)}, u32[]{:S(2)}) async-start(bf16[8,128,256]{1,2,0:T(8,128)(2,1)} %copy.73), calls=%async_computation.4 | async-start | bytes 1048576 | tf_op jit(solution)/shard_map/all_to_all | solution.py:103
  315.2 22.6 %all-to-all-start.5 = ((bf16[8,128,256]{1,2,0:T(8,128)(2,1)}), bf16[8,128,256]{1,2,0:T(8,128)(2,1)S(1)}, u32[]{:S(2)}, u32[]{:S(2)}) async-start(bf16[8,128,256]{1,2,0:T(8,128)(2,1)} %copy.75), calls=%async_computation.5 | async-start | bytes 1048576 | tf_op jit(solution)/shard_map/all_to_all | solution.py:104
  337.8 26.7 %all-to-all-start.6 = ((bf16[32,96,256]{2,1,0:T(8,128)(2,1)}), bf16[32,96,256]{2,1,0:T(8,128)(2,1)S(1)}, u32[]{:S(2)}, u32[]{:S(2)}) async-start(bf16[32,96,256]{2,1,0:T(8,128)(2,1)} %bitcast.22), calls=%async_computation.6 | async-start | bytes 3145728 | tf_op jit(solution)/shard_map/all_to_all | solution.py:98
Sparse Core Ops, SparseCore 0:
  10.4 151.3 all-gather.2
  163.7 86.9 all-gather.4

commit v2 on v1

v2 whole, which is shorter than its diff:
```python
import functools
import math

import jax
import jax.numpy as jnp
from jax import lax
from jax.experimental import pallas as pl
from jax.experimental.pallas import tpu as pltpu
from jax.sharding import PartitionSpec as P

HEAD_DIM = 128
VIEW_TOK = 64
HEADS_HERE = 2
BF16 = jnp.bfloat16
F32 = jnp.float32
MESH = pl.DeviceIdType.MESH


def slot_objects(counts, slots):
    count_ends = jnp.cumsum(counts)
    view_order = jnp.arange(slots.shape[0], dtype=jnp.int32)
    view_object = jnp.sum((view_order[:, None] >= count_ends[None, :]).astype(jnp.int32), axis=1)
    placed = slots[:, None] == view_order[None, :]
    return jnp.sum(jnp.where(placed, view_object[:, None], 0), axis=0)


def dot(a, b, contract):
    return lax.dot_general(a, b, ((contract[:1], contract[1:]), ((), ())), preferred_element_type=F32)


def kernel(
    dims,
    slot_obj,
    key_obj,
    g_in,
    q_in,
    k_in,
    v_in,
    w_in,
    dq_out,
    dk_out,
    dv_out,
    gp_out,
    g_all,
    w_all,
    qkv,
    qkv_relay,
    probs,
    att,
    dk_acc,
    dv_acc,
    d_send,
    d_relay,
    gp_acc,
    gp_send,
    gp_recv,
    gp_sum,
    gp_pair,
    gp_land,
    g_recv_sem,
    g_send_sem,
    g_fwd_sem,
    w_recv_sem,
    w_send_sem,
    w_fwd_sem,
    qkv_recv_sem,
    qkv_send_sem,
    relay_recv_sem,
    relay_fwd_sem,
    d_recv_sem,
    d_send_sem,
    d_relay_sem,
    d_fwd_sem,
    rs_send_sem,
    rs_recv_sem,
    pair_sem,
    land_send_sem,
    land_recv_sem,
):
    planes, rows, width, piece = dims
    half = rows // 2
    chip_rows = 2 * rows
    tokens = 8 * rows
    scale = 1.0 / math.sqrt(HEAD_DIM)
    dp = lax.axis_index("dp")
    cam = lax.axis_index("cam")
    spot, z_lo = dp // 2, dp % 2
    pair = spot * 2 + (1 - z_lo)
    chip, core = cam // 2, cam % 2
    ahead, behind, across = (chip + 1) % 4, (chip + 3) % 4, (chip + 2) % 4
    sibling = chip * 2 + (1 - core)
    outs = (dq_out, dk_out, dv_out)
    ins = (q_in, k_in, v_in)

    def block(index):
        return pl.ds(pl.multiple_of(index * rows, rows), rows)

    def cols(index):
        return pl.ds(pl.multiple_of(index * width, width), width)

    def remote(src, dst, send, recv, **where):
        return pltpu.make_async_remote_copy(
            src_ref=src, dst_ref=dst, send_sem=send, recv_sem=recv, device_id=where, device_id_type=MESH
        )

    def arrived(ref, sem):
        pltpu.make_async_copy(ref, ref, sem).wait()

    def in_plane(step):
        return (spot + step) % planes

    barrier = pltpu.get_barrier_semaphore()

    @pl.loop(1, planes)
    def _(step):
        pl.semaphore_signal(barrier, inc=1, device_id={"dp": in_plane(step) * 2 + z_lo}, device_id_type=MESH)

    pl.semaphore_signal(barrier, inc=1, device_id={"dp": pair}, device_id_type=MESH)

    @pl.loop(1, 8)
    def _(step):
        pl.semaphore_signal(barrier, inc=1, device_id={"cam": (cam + step) % 8}, device_id_type=MESH)

    pl.semaphore_wait(barrier, planes + 7)

    def qkv_copy(j, dst_cam, slot):
        return remote(
            ins[j].at[:, cols(dst_cam)],
            qkv.at[j, block(cam), :],
            qkv_send_sem.at[slot, j],
            qkv_recv_sem.at[cam, j],
            cam=dst_cam,
        )

    def qkv_far(j, way):
        return remote(
            ins[j].at[:, cols(across * 2 + way)],
            qkv_relay.at[way, j],
            qkv_send_sem.at[5 + way, j],
            relay_recv_sem.at[way, j],
            cam=(ahead, behind)[way] * 2 + core,
        )

    def qkv_forward(j, way):
        source = (behind, ahead)[way] * 2 + core
        return remote(
            qkv_relay.at[way, j],
            qkv.at[j, block(source), :],
            relay_fwd_sem.at[way, j],
            qkv_recv_sem.at[source, j],
            cam=(ahead, behind)[way] * 2 + way,
        )

    near = (ahead * 2, behind * 2, ahead * 2 + 1, behind * 2 + 1, sibling)
    for j in range(3):
        for way in range(2):
            qkv_far(j, way).start()
        for slot in range(5):
            qkv_copy(j, near[slot], slot).start()
        pltpu.make_async_copy(
            ins[j].at[:, cols(cam)], qkv.at[j, block(cam), :], qkv_recv_sem.at[cam, j]
        ).start()

    def w_rows(index):
        return pl.ds(pl.multiple_of(index * piece, piece), piece)

    def w_copy(dst_dp, sem):
        return remote(w_in.at[:, cols(cam)], w_all.at[w_rows(dp), :], sem, w_recv_sem.at[dp], dp=dst_dp)

    def w_forward(step):
        return remote(
            w_all.at[w_rows(pair), :],
            w_all.at[w_rows(pair), :],
            w_fwd_sem.at[step],
            w_recv_sem.at[pair],
            dp=in_plane(step) * 2 + z_lo,
        )

    w_copy(pair, w_send_sem.at[0]).start()
    pltpu.make_async_copy(w_in.at[:, cols(cam)], w_all.at[w_rows(dp), :], w_recv_sem.at[dp]).start()

    @pl.loop(1, planes)
    def _(step):
        w_copy(in_plane(step) * 2 + z_lo, w_send_sem.at[step]).start()

    def g_part(index, part):
        return pl.ds(pl.multiple_of(index * rows + part * half, half), half)

    def g_own(part, slot, dst_cam):
        return remote(
            g_in.at[part * half : (part + 1) * half, :],
            g_all.at[g_part(cam, part), :],
            g_send_sem.at[slot, part],
            g_recv_sem.at[cam, part],
            cam=dst_cam,
        )

    def g_pass(source, part, sem, dst_cam):
        here = g_all.at[g_part(source, part), :]
        return remote(here, here, sem, g_recv_sem.at[source, part], cam=dst_cam)

    def g_local(part):
        return pltpu.make_async_copy(
            g_in.at[part * half : (part + 1) * half, :],
            g_all.at[g_part(cam, part), :],
            g_recv_sem.at[cam, part],
        )

    def g_wait(source, part):
        arrived(g_all.at[g_part(source, part), :], g_recv_sem.at[source, part])

    g_near = (ahead * 2 + core, behind * 2 + core, sibling)

    def g_start():
        for part in range(2):
            g_own(part, 0, g_near[0]).start()
            g_own(1 - part, 1, g_near[1]).start()
            g_own(part, 2, g_near[2]).start()
            g_local(part).start()

    g_start()

    arrived(w_all.at[w_rows(pair), :], w_recv_sem.at[pair])

    @pl.loop(1, planes)
    def _(step):
        w_forward(step).start()

    for j in range(3):
        for way in range(2):
            arrived(qkv_relay.at[way, j], relay_recv_sem.at[way, j])
            qkv_forward(j, way).start()

    for j in range(3):

        @pl.loop(0, 8)
        def _(source):
            arrived(qkv.at[j, block(source), :], qkv_recv_sem.at[source, j])

    dk_acc[...] = jnp.zeros_like(dk_acc)
    dv_acc[...] = jnp.zeros_like(dv_acc)
    gp_acc[...] = jnp.zeros_like(gp_acc)

    @pl.loop(0, 8)
    def _(r):
        here = block(r)
        row = lax.broadcasted_iota(jnp.int32, (rows, 1), 0)
        row_obj = jnp.where(row < VIEW_TOK, slot_obj[r * 2], slot_obj[r * 2 + 1])
        same = row_obj == key_obj[...]
        for i in range(HEADS_HERE):
            head = slice(i * HEAD_DIM, (i + 1) * HEAD_DIM)
            scores = dot(qkv[0, here, head], qkv[1, :, head], (1, 1)) * scale
            scores = jnp.where(same, scores, -jnp.inf)
            exps = jnp.exp(scores - jnp.max(scores, axis=1, keepdims=True))
            p = exps * (1.0 / jnp.sum(exps, axis=1, keepdims=True))
            probs[i, here, :] = p
            att[here, head] = dot(p.astype(BF16), qkv[2, :, head], (1, 0))

    @pl.loop(0, planes * 2)
    def _(source):
        @pl.when(source != pair)
        def _():
            arrived(w_all.at[w_rows(source), :], w_recv_sem.at[source])

    def d_direct(j, dst_cam, slot):
        return remote(
            d_send.at[j, block(dst_cam), :],
            outs[j].at[:, cols(cam)],
            d_send_sem.at[slot, j],
            d_recv_sem.at[cam, j],
            cam=dst_cam,
        )

    def d_far(j, way):
        return remote(
            d_send.at[j, block(across * 2 + way), :],
            d_relay.at[way, j],
            d_send_sem.at[5 + way, j],
            d_relay_sem.at[way, j],
            cam=(ahead, behind)[way] * 2 + core,
        )

    def d_forward(j, way):
        source = (behind, ahead)[way] * 2 + core
        return remote(
            d_relay.at[way, j],
            outs[j].at[:, cols(source)],
            d_fwd_sem.at[way, j],
            d_recv_sem.at[source, j],
            cam=(ahead, behind)[way] * 2 + way,
        )

    def d_local(j):
        return pltpu.make_async_copy(
            d_send.at[j, block(cam), :], outs[j].at[:, cols(cam)], d_recv_sem.at[cam, j]
        )

    def g_tile(j):
        return pl.ds(pl.multiple_of(j * 4 * piece, 128), 4 * piece)

    @pl.loop(0, 4)
    def _(t):
        step = jnp.where(t == 0, 0, jnp.where(t == 1, 3, jnp.where(t == 2, 1, 2)))
        c = (chip + step) % 4

        @pl.when(t == 1)
        def _():
            back, front = behind * 2 + core, ahead * 2 + core
            g_wait(back, 0)
            g_pass(back, 0, g_fwd_sem.at[0, 0], front).start()
            g_pass(back, 0, g_fwd_sem.at[1, 0], sibling).start()
            g_wait(front, 1)
            g_pass(front, 1, g_fwd_sem.at[0, 1], back).start()
            g_pass(front, 1, g_fwd_sem.at[2, 1], sibling).start()
            g_wait(back, 1)
            g_pass(back, 1, g_fwd_sem.at[1, 1], sibling).start()
            g_wait(front, 0)
            g_pass(front, 0, g_fwd_sem.at[2, 0], sibling).start()

        @pl.when(t == 3)
        def _():
            for part in range(2):
                g_wait(across * 2 + core, part)
                g_pass(across * 2 + core, part, g_fwd_sem.at[3, part], sibling).start()

        @pl.when(t == 0)
        def _():
            for part in range(2):
                g_wait(cam, part)

        for part in range(2):
            g_wait(c * 2 + 1 - core, part)

        here = pl.ds(pl.multiple_of(c * chip_rows, chip_rows), chip_rows)
        grad_att = dot(g_all[here, :], w_all[...], (1, 0)).astype(BF16)
        for i in range(HEADS_HERE):
            head = slice(i * HEAD_DIM, (i + 1) * HEAD_DIM)
            go = grad_att[:, head]
            p = probs[i, here, :]
            delta = jnp.sum(go.astype(F32) * att[here, head], axis=1, keepdims=True)
            ds = (p * (dot(go, qkv[2, :, head], (1, 1)) - delta)).astype(BF16)
            d_send[0, here, head] = (dot(ds, qkv[1, :, head], (1, 0)) * scale).astype(BF16)
            dk_acc[:, head] += dot(ds, qkv[0, here, head], (0, 0))
            dv_acc[:, head] += dot(p.astype(BF16), go, (0, 0))

        @pl.when(t == 0)
        def _():
            d_local(0).start()
            d_direct(0, sibling, 4).start()

        @pl.when(t == 1)
        def _():
            d_direct(0, behind * 2, 1).start()
            d_direct(0, behind * 2 + 1, 3).start()

        @pl.when(t == 2)
        def _():
            d_direct(0, ahead * 2, 0).start()
            d_direct(0, ahead * 2 + 1, 2).start()

        @pl.when(t < 3)
        def _():
            att_here = att[here, :].astype(BF16)

            @pl.loop(0, planes // 2)
            def _(j):
                gp_acc[g_tile(j), :] += dot(g_all[here, g_tile(j)], att_here, (0, 0))

    d_send[1] = (dk_acc[...] * scale).astype(BF16)
    d_send[2] = dv_acc[...].astype(BF16)
    for j in range(3):
        for way in range(2):
            d_far(j, way).start()
    for j in range(1, 3):
        for slot in range(5):
            d_direct(j, near[slot], slot).start()
        d_local(j).start()

    def two(index):
        return pl.ds(pl.multiple_of(index * 2 * piece, 2 * piece), 2 * piece)

    def rs_copy(peer):
        return remote(
            gp_send.at[two(peer), :],
            gp_recv.at[spot],
            rs_send_sem.at[peer],
            rs_recv_sem.at[spot],
            dp=peer * 2 + z_lo,
        )

    last = pl.ds(pl.multiple_of(across * chip_rows, chip_rows), chip_rows)
    att_last = att[last, :].astype(BF16)

    @pl.loop(0, planes // 2)
    def _(jj):
        j = (spot // 2 + jj) % (planes // 2)
        total = gp_acc[g_tile(j), :] + dot(g_all[last, g_tile(j)], att_last, (0, 0))
        gp_acc[g_tile(j), :] = total
        gp_send[g_tile(j), :] = total.astype(BF16)
        for side in range(2):
            peer = j * 2 + side

            @pl.when(peer != spot)
            def _():
                rs_copy(peer).start()

    for j in range(3):
        for way in range(2):
            arrived(d_relay.at[way, j], d_relay_sem.at[way, j])
            d_forward(j, way).start()

    gp_sum[...] = gp_acc[two(spot), :]

    @pl.loop(1, planes)
    def _(step):
        peer = (spot + planes - step) % planes
        arrived(gp_recv.at[peer], rs_recv_sem.at[peer])
        gp_sum[...] += gp_recv[peer].astype(F32)

    def own_half(side):
        return pl.ds(pl.multiple_of(side * piece, piece), piece)

    pair_copy = remote(
        gp_sum.at[own_half(1 - z_lo), :], gp_pair, pair_sem.at[0], pair_sem.at[1], dp=pair
    )
    pair_copy.start()
    pair_copy.wait()
    gp_land[cam] = (gp_sum[own_half(z_lo), :] + gp_pair[...]).astype(BF16)

    def land_copy(step):
        return remote(
            gp_land.at[cam],
            gp_land.at[cam],
            land_send_sem.at[step],
            land_recv_sem.at[cam],
            cam=(cam + step) % 8,
        )

    @pl.loop(1, 8)
    def _(step):
        land_copy(step).start()

    @pl.loop(1, 8)
    def _(step):
        source = (cam + 8 - step) % 8
        arrived(gp_land.at[source], land_recv_sem.at[source])

    for source in range(8):
        gp_out[:, source * width : (source + 1) * width] = gp_land[source].astype(F32)

    for j in range(3):

        @pl.loop(0, 8)
        def _(source):
            arrived(outs[j].at[:, cols(source)], d_recv_sem.at[source, j])

    for j in range(3):
        for slot in range(5):
            qkv_copy(j, near[slot], slot).wait_send()
            d_direct(j, near[slot], slot).wait_send()
        for way in range(2):
            qkv_far(j, way).wait_send()
            qkv_forward(j, way).wait_send()
            d_far(j, way).wait_send()
            d_forward(j, way).wait_send()
    w_copy(pair, w_send_sem.at[0]).wait_send()

    @pl.loop(1, planes)
    def _(step):
        w_copy(in_plane(step) * 2 + z_lo, w_send_sem.at[step]).wait_send()
        w_forward(step).wait_send()
        rs_copy(in_plane(step)).wait_send()

    for part in range(2):
        for slot in range(3):
            g_own(part, slot, g_near[slot]).wait_send()
        for slot in range(4):
            g_pass(cam, part, g_fwd_sem.at[slot, part], sibling).wait_send()

    @pl.loop(1, 8)
    def _(step):
        land_copy(step).wait_send()


def local(grad_out, query_act, key_act, value_act, out_proj, view_counts, view_slots):
    rows, model = grad_out.shape
    devices_dp = lax.axis_size("dp")
    planes = devices_dp // 2
    piece = out_proj.shape[0]
    width = query_act.shape[1] // 8
    tokens = rows * 8
    slot_obj = slot_objects(view_counts[0], view_slots[0])
    key_obj = jnp.repeat(slot_obj, VIEW_TOK)[None, :]
    dims = (planes, rows, width, piece)
    any_spec = pl.BlockSpec(memory_space=pl.ANY)
    dma = pltpu.SemaphoreType.DMA
    gradient = jax.ShapeDtypeStruct(query_act.shape, BF16)
    return pl.pallas_call(
        functools.partial(kernel, dims),
        out_shape=(gradient, gradient, gradient, jax.ShapeDtypeStruct((piece, width * 8), F32)),
        in_specs=[pl.BlockSpec(memory_space=pltpu.SMEM), pl.BlockSpec(memory_space=pltpu.VMEM)]
        + [any_spec] * 5,
        out_specs=(any_spec, any_spec, any_spec, pl.BlockSpec(memory_space=pltpu.VMEM)),
        scratch_shapes=[
            pltpu.VMEM((tokens, model), BF16),
            pltpu.VMEM((model, width), BF16),
            pltpu.VMEM((3, tokens, width), BF16),
            pltpu.VMEM((2, 3, rows, width), BF16),
            pltpu.VMEM((HEADS_HERE, tokens, tokens), F32),
            pltpu.VMEM((tokens, width), F32),
            pltpu.VMEM((tokens, width), F32),
            pltpu.VMEM((tokens, width), F32),
            pltpu.VMEM((3, tokens, width), BF16),
            pltpu.VMEM((2, 3, rows, width), BF16),
            pltpu.VMEM((model, width), F32),
            pltpu.VMEM((model, width), BF16),
            pltpu.VMEM((planes, 2 * piece, width), BF16),
            pltpu.VMEM((2 * piece, width), F32),
            pltpu.VMEM((piece, width), F32),
            pltpu.VMEM((8, piece, width), BF16),
            dma((8, 2)),
            dma((3, 2)),
            dma((4, 2)),
            dma((devices_dp,)),
            dma((planes,)),
            dma((planes,)),
            dma((8, 3)),
            dma((7, 3)),
            dma((2, 3)),
            dma((2, 3)),
            dma((8, 3)),
            dma((7, 3)),
            dma((2, 3)),
            dma((2, 3)),
            dma((planes,)),
            dma((planes,)),
            dma((2,)),
            dma((8,)),
            dma((8,)),
        ],
        compiler_params=pltpu.CompilerParams(
            collective_id=0, has_side_effects=True, vmem_limit_bytes=60 * 1024 * 1024
        ),
        name="group_backward",
    )(slot_obj, key_obj, grad_out, query_act, key_act, value_act, out_proj)


def solution(mesh):
    rows = P(("dp", "cam"), None)
    in_specs = (rows, rows, rows, rows, P("dp", None), P("dp", None), P("dp", None))
    out_specs = (rows, rows, rows, P("dp", None))
    return jax.shard_map(local, mesh=mesh, in_specs=in_specs, out_specs=out_specs, check_vma=False)
```

time: 395 us -> 177 us (0.45)
  waiting for transfers between devices: 270 us -> 0 us
  Pallas kernels: 0 us -> 167 us
  starting transfers between devices: 42.5 us -> 0 us
  blocking collectives: 21.2 us -> 0 us
  matrix products: 20.1 us -> 0 us
  between operations: 14.2 us -> 0.67 us
  local copies, waits for them, and re-layouts: 19.1 us -> 6.84 us
  other arithmetic: 5.62 us -> 0.35 us
    all_gather x2 -> x0, waiting for transfers between devices: 182 us -> none  [the longest x1 92.7 us: local(): out_columns = lax.all_gather(out_columns, 'dp', axis=0, tiled=True)]
    pallas_call x0 -> x1, Pallas kernels: none -> 167 us  [local(): pl.pallas_call(functools.partial(kernel, dims), out_shape=(gradient, grad...]
    all_to_all x7 -> x0, waiting for transfers between devices: 87.3 us -> none  [the longest x1 19.7 us: local(): lax.all_to_all(key_act, 'cam', split_axis=1, concat_axis=0, tiled=True)]
    all_to_all x7 -> x0, starting transfers between devices: 42.4 us -> none  [the longest x1 9.97 us: local(): lax.all_to_all(query_act, 'cam', split_axis=1, concat_axis=0, tiled=True)]
    all_gather x1 -> x0, blocking collectives: 21.2 us -> none  [local(): grad_proj = lax.all_gather(partial_rows, 'cam', axis=1, tiled=True)]
    dot_general x14 -> x0, matrix products: 20.1 us -> none  [the longest x1 5.11 us: local(): jnp.dot(whole_out, out_columns, preferred_element_type=jnp.float32)]
    all_to_all x6 -> x0, local copies, waits for them, and re-layouts: 7.21 us -> none  [the longest x1 1.87 us: local(): lax.all_to_all(query_act, 'cam', split_axis=1, concat_axis=0, tiled=True)]
  transfers between devices with their start and end apart: 9 -> 0, of which waited for: 8 -> 0; matrix products, arithmetic and copies ran while one was open for 6% -> 0% of each run, Pallas kernels for 0% -> 0%
where the time goes in v2:
time: 177 us; the launch traced here: 174 us
  Pallas kernels  167 us (94%)
  local copies, waits for them, and re-layouts  6.84 us (4%)
    pallas_call x1, Pallas kernels, local(): pl.pallas_call(functools.partial(kernel, dims), out_shape=(gradient, grad...  167 us
    unnamed x16, local copies, waits for them, and re-layouts  6.1 us

profile of v2, /device:TPU:1, one launch (start us, length us, event | category | flops | bytes accessed | tf_op | source)
XLA Modules:
  0.0 174.4 jit_solution(9645338296451681146)
XLA Ops:
  0.6 0.0 copy-start.4
  0.6 0.6 copy-done.4
  1.3 0.2 reduce-window.8
  1.5 0.0 copy-start.5
  1.5 0.1 convert_reduce_fusion
  1.6 0.6 copy-done.5
  2.1 0.1 select_reduce_fusion.slot_obj
  2.2 0.0 copy-start.3
  2.2 0.1 broadcast_in_dim.21
  2.3 0.4 copy-done.3
  2.7 0.7 broadcast_in_dim_reshape.3.key_obj
  3.4 166.5 %group_backward.1 = (bf16[128,2048]{1,0:T(8,128)(2,1)}, bf16[128,2048]{1,0:T(8,128)(2,1)}, bf16[128,2048]{1,0:T(8,128)(2,1)}, f32[96,2048]{1,0:T(8,128)}) custom-call(s32[16]{0:T(128)} %copy-done.3, s32[1,1024]{1,0:T(1,128)} %broadcast_in_dim_reshape.3.key_obj, bf16[128,3072]{1,0:T(8,128)(2,1)} %g_in.1, bf16[128,2048]{1,0:T(8,128)(2,1)} %q_in.1, ...), custom_call_target="tpu_custom_call" | custom-call | tf_op jit(solution)/shard_map/group_backward/pallas_call | solution.py:498
  169.9 0.0 copy-start.2
  169.9 0.0 copy-start.1
  170.0 2.0 %copy.15 = bf16[128,2048]{1,0:T(8,128)(2,1)} copy(bf16[128,2048]{1,0:T(8,128)(2,1)} %get-tuple-element.8) | data formatting | bytes 1048576
  171.9 0.0 copy-done.2
  171.9 0.0 copy-start
  171.9 0.8 copy.16
  172.7 0.0 copy-done.1
  172.7 0.8 copy.17
  173.5 0.0 copy-done
  173.5 0.9 copy.18
Async XLA Ops:
  0.6 0.7 copy-start.4
  1.5 0.7 copy-start.5
  2.2 0.5 copy-start.3
  169.9 2.0 %copy-start.2 = (bf16[128,2048]{1,0:T(8,128)(2,1)S(1)}, bf16[128,2048]{1,0:T(8,128)(2,1)}, u32[]{:S(2)}) copy-start(bf16[128,2048]{1,0:T(8,128)(2,1)} %get-tuple-element.9) | copy-start | bytes 1572868
  169.9 2.8 %copy-start.1 = (bf16[128,2048]{1,0:T(8,128)(2,1)S(1)}, bf16[128,2048]{1,0:T(8,128)(2,1)}, u32[]{:S(2)}) copy-start(bf16[128,2048]{1,0:T(8,128)(2,1)} %get-tuple-element.10) | copy-start | bytes 1572868
  171.9 1.6 copy-start

commit v3 on v2

--- a/solution.py
+++ b/solution.py
@@ -16,22 +16,14 @@
 MESH = pl.DeviceIdType.MESH
 
 
-def slot_objects(counts, slots):
-    count_ends = jnp.cumsum(counts)
-    view_order = jnp.arange(slots.shape[0], dtype=jnp.int32)
-    view_object = jnp.sum((view_order[:, None] >= count_ends[None, :]).astype(jnp.int32), axis=1)
-    placed = slots[:, None] == view_order[None, :]
-    return jnp.sum(jnp.where(placed, view_object[:, None], 0), axis=0)
-
-
 def dot(a, b, contract):
     return lax.dot_general(a, b, ((contract[:1], contract[1:]), ((), ())), preferred_element_type=F32)
 
 
 def kernel(
     dims,
-    slot_obj,
-    key_obj,
+    counts,
+    slots,
     g_in,
     q_in,
     k_in,
@@ -40,23 +32,23 @@
     dq_out,
     dk_out,
     dv_out,
-    gp_out,
+    land_out,
     g_all,
     w_all,
     qkv,
-    qkv_relay,
     probs,
     att,
     dk_acc,
     dv_acc,
     d_send,
-    d_relay,
     gp_acc,
     gp_send,
     gp_recv,
     gp_sum,
     gp_pair,
-    gp_land,
+    gp_last,
+    slot_obj,
+    key_obj,
     g_recv_sem,
     g_send_sem,
     g_fwd_sem,
@@ -65,12 +57,8 @@
     w_fwd_sem,
     qkv_recv_sem,
     qkv_send_sem,
-    relay_recv_sem,
-    relay_fwd_sem,
     d_recv_sem,
     d_send_sem,
-    d_relay_sem,
-    d_fwd_sem,
     rs_send_sem,
     rs_recv_sem,
     pair_sem,
@@ -132,31 +120,10 @@
             cam=dst_cam,
         )
 
-    def qkv_far(j, way):
-        return remote(
-            ins[j].at[:, cols(across * 2 + way)],
-            qkv_relay.at[way, j],
-            qkv_send_sem.at[5 + way, j],
-            relay_recv_sem.at[way, j],
-            cam=(ahead, behind)[way] * 2 + core,
-        )
-
-    def qkv_forward(j, way):
-        source = (behind, ahead)[way] * 2 + core
-        return remote(
-            qkv_relay.at[way, j],
-            qkv.at[j, block(source), :],
-            relay_fwd_sem.at[way, j],
-            qkv_recv_sem.at[source, j],
-            cam=(ahead, behind)[way] * 2 + way,
-        )
-
-    near = (ahead * 2, behind * 2, ahead * 2 + 1, behind * 2 + 1, sibling)
+    others = (across * 2, across * 2 + 1, ahead * 2, behind * 2, ahead * 2 + 1, behind * 2 + 1, sibling)
     for j in range(3):
-        for way in range(2):
-            qkv_far(j, way).start()
-        for slot in range(5):
-            qkv_copy(j, near[slot], slot).start()
+        for slot in range(7):
+            qkv_copy(j, others[slot], slot).start()
         pltpu.make_async_copy(
             ins[j].at[:, cols(cam)], qkv.at[j, block(cam), :], qkv_recv_sem.at[cam, j]
         ).start()
@@ -218,18 +185,34 @@
             g_own(part, 2, g_near[2]).start()
             g_local(part).start()
 
-    g_start()
+
+    ends = [counts[0, 0]]
+    for o in range(1, counts.shape[1]):
+        ends.append(ends[-1] + counts[0, o])
+    views = slots.shape[1]
+    view_obj = [sum((v >= end).astype(jnp.int32) for end in ends) for v in range(views)]
+
+    @pl.loop(0, views)
+    def _(s):
+        found = jnp.int32(0)
+        for v in range(views):
+            found = found + jnp.where(slots[0, v] == s, view_obj[v], 0)
+        slot_obj[s] = found
+
+    lane_slot = lax.broadcasted_iota(jnp.int32, (1, tokens), 1) // VIEW_TOK
+    lane_obj = jnp.zeros((1, tokens), jnp.int32)
+    for s in range(views):
+        lane_obj = jnp.where(lane_slot == s, slot_obj[s], lane_obj)
+    key_obj[...] = lane_obj
+    dk_acc[...] = jnp.zeros_like(dk_acc)
+    dv_acc[...] = jnp.zeros_like(dv_acc)
+    gp_acc[...] = jnp.zeros_like(gp_acc)
 
     arrived(w_all.at[w_rows(pair), :], w_recv_sem.at[pair])
 
     @pl.loop(1, planes)
     def _(step):
         w_forward(step).start()
-
-    for j in range(3):
-        for way in range(2):
-            arrived(qkv_relay.at[way, j], relay_recv_sem.at[way, j])
-            qkv_forward(j, way).start()
 
     for j in range(3):
 
@@ -237,9 +220,8 @@
         def _(source):
             arrived(qkv.at[j, block(source), :], qkv_recv_sem.at[source, j])
 
-    dk_acc[...] = jnp.zeros_like(dk_acc)
-    dv_acc[...] = jnp.zeros_like(dv_acc)
-    gp_acc[...] = jnp.zeros_like(gp_acc)
+    g_start()
+
 
     @pl.loop(0, 8)
     def _(r):
@@ -271,25 +253,6 @@
             cam=dst_cam,
         )
 
-    def d_far(j, way):
-        return remote(
-            d_send.at[j, block(across * 2 + way), :],
-            d_relay.at[way, j],
-            d_send_sem.at[5 + way, j],
-            d_relay_sem.at[way, j],
-            cam=(ahead, behind)[way] * 2 + core,
-        )
-
-    def d_forward(j, way):
-        source = (behind, ahead)[way] * 2 + core
-        return remote(
-            d_relay.at[way, j],
-            outs[j].at[:, cols(source)],
-            d_fwd_sem.at[way, j],
-            d_recv_sem.at[source, j],
-            cam=(ahead, behind)[way] * 2 + way,
-        )
-
     def d_local(j):
         return pltpu.make_async_copy(
             d_send.at[j, block(cam), :], outs[j].at[:, cols(cam)], d_recv_sem.at[cam, j]
@@ -346,17 +309,17 @@
         @pl.when(t == 0)
         def _():
             d_local(0).start()
-            d_direct(0, sibling, 4).start()
+            d_direct(0, sibling, 6).start()
 
         @pl.when(t == 1)
         def _():
-            d_direct(0, behind * 2, 1).start()
-            d_direct(0, behind * 2 + 1, 3).start()
+            d_direct(0, behind * 2, 3).start()
+            d_direct(0, behind * 2 + 1, 5).start()
 
         @pl.when(t == 2)
         def _():
-            d_direct(0, ahead * 2, 0).start()
-            d_direct(0, ahead * 2 + 1, 2).start()
+            d_direct(0, ahead * 2, 2).start()
+            d_direct(0, ahead * 2 + 1, 4).start()
 
         @pl.when(t < 3)
         def _():
@@ -369,12 +332,10 @@
     d_send[1] = (dk_acc[...] * scale).astype(BF16)
     d_send[2] = dv_acc[...].astype(BF16)
     for j in range(3):
-        for way in range(2):
-            d_far(j, way).start()
-    for j in range(1, 3):
-        for slot in range(5):
-            d_direct(j, near[slot], slot).start()
-        d_local(j).start()
+        for slot in range(2 if j == 0 else 7):
+            d_direct(j, others[slot], slot).start()
+        if j > 0:
+            d_local(j).start()
 
     def two(index):
         return pl.ds(pl.multiple_of(index * 2 * piece, 2 * piece), 2 * piece)
@@ -404,11 +365,6 @@
             def _():
                 rs_copy(peer).start()
 
-    for j in range(3):
-        for way in range(2):
-            arrived(d_relay.at[way, j], d_relay_sem.at[way, j])
-            d_forward(j, way).start()
-
     gp_sum[...] = gp_acc[two(spot), :]
 
     @pl.loop(1, planes)
@@ -425,28 +381,26 @@
     )
     pair_copy.start()
     pair_copy.wait()
-    gp_land[cam] = (gp_sum[own_half(z_lo), :] + gp_pair[...]).astype(BF16)
+    gp_last[...] = (gp_sum[own_half(z_lo), :] + gp_pair[...]).astype(BF16)
 
     def land_copy(step):
         return remote(
-            gp_land.at[cam],
-            gp_land.at[cam],
+            gp_last,
+            land_out.at[cam],
             land_send_sem.at[step],
             land_recv_sem.at[cam],
             cam=(cam + step) % 8,
         )
 
+    pltpu.make_async_copy(gp_last, land_out.at[cam], land_recv_sem.at[cam]).start()
+
     @pl.loop(1, 8)
     def _(step):
         land_copy(step).start()
 
-    @pl.loop(1, 8)
-    def _(step):
-        source = (cam + 8 - step) % 8
-        arrived(gp_land.at[source], land_recv_sem.at[source])
-
-    for source in range(8):
-        gp_out[:, source * width : (source + 1) * width] = gp_land[source].astype(F32)
+    @pl.loop(0, 8)
+    def _(source):
+        arrived(land_out.at[source], land_recv_sem.at[source])
 
     for j in range(3):
 
@@ -455,14 +409,9 @@
             arrived(outs[j].at[:, cols(source)], d_recv_sem.at[source, j])
 
     for j in range(3):
-        for slot in range(5):
-            qkv_copy(j, near[slot], slot).wait_send()
-            d_direct(j, near[slot], slot).wait_send()
-        for way in range(2):
-            qkv_far(j, way).wait_send()
-            qkv_forward(j, way).wait_send()
-            d_far(j, way).wait_send()
-            d_forward(j, way).wait_send()
+        for slot in range(7):
+            qkv_copy(j, others[slot], slot).wait_send()
+            d_direct(j, others[slot], slot).wait_send()
     w_copy(pair, w_send_sem.at[0]).wait_send()
 
     @pl.loop(1, planes)
@@ -489,35 +438,33 @@
     piece = out_proj.shape[0]
     width = query_act.shape[1] // 8
     tokens = rows * 8
-    slot_obj = slot_objects(view_counts[0], view_slots[0])
-    key_obj = jnp.repeat(slot_obj, VIEW_TOK)[None, :]
     dims = (planes, rows, width, piece)
     any_spec = pl.BlockSpec(memory_space=pl.ANY)
     dma = pltpu.SemaphoreType.DMA
     gradient = jax.ShapeDtypeStruct(query_act.shape, BF16)
-    return pl.pallas_call(
+    *gradients, land = pl.pallas_call(
         functools.partial(kernel, dims),
-        out_shape=(gradient, gradient, gradient, jax.ShapeDtypeStruct((piece, width * 8), F32)),
-        in_specs=[pl.BlockSpec(memory_space=pltpu.SMEM), pl.BlockSpec(memory_space=pltpu.VMEM)]
+        out_shape=(gradient, gradient, gradient, jax.ShapeDtypeStruct((8, piece, width), BF16)),
+        in_specs=[pl.BlockSpec(memory_space=pltpu.SMEM)] * 2
         + [any_spec] * 5,
-        out_specs=(any_spec, any_spec, any_spec, pl.BlockSpec(memory_space=pltpu.VMEM)),
+        out_specs=(any_spec,) * 4,
         scratch_shapes=[
             pltpu.VMEM((tokens, model), BF16),
             pltpu.VMEM((model, width), BF16),
             pltpu.VMEM((3, tokens, width), BF16),
-            pltpu.VMEM((2, 3, rows, width), BF16),
             pltpu.VMEM((HEADS_HERE, tokens, tokens), F32),
             pltpu.VMEM((tokens, width), F32),
             pltpu.VMEM((tokens, width), F32),
             pltpu.VMEM((tokens, width), F32),
             pltpu.VMEM((3, tokens, width), BF16),
-            pltpu.VMEM((2, 3, rows, width), BF16),
             pltpu.VMEM((model, width), F32),
             pltpu.VMEM((model, width), BF16),
             pltpu.VMEM((planes, 2 * piece, width), BF16),
             pltpu.VMEM((2 * piece, width), F32),
             pltpu.VMEM((piece, width), F32),
-            pltpu.VMEM((8, piece, width), BF16),
+            pltpu.VMEM((piece, width), BF16),
+            pltpu.SMEM((view_slots.shape[1],), jnp.int32),
+            pltpu.VMEM((1, tokens), jnp.int32),
             dma((8, 2)),
             dma((3, 2)),
             dma((4, 2)),
@@ -526,12 +473,8 @@
             dma((planes,)),
             dma((8, 3)),
             dma((7, 3)),
-            dma((2, 3)),
-            dma((2, 3)),
             dma((8, 3)),
             dma((7, 3)),
-            dma((2, 3)),
-            dma((2, 3)),
             dma((planes,)),
             dma((planes,)),
             dma((2,)),
@@ -542,7 +485,33 @@
             collective_id=0, has_side_effects=True, vmem_limit_bytes=60 * 1024 * 1024
         ),
         name="group_backward",
-    )(slot_obj, key_obj, grad_out, query_act, key_act, value_act, out_proj)
+    )(view_counts, view_slots, grad_out, query_act, key_act, value_act, out_proj)
+
+    vmem = pl.BlockSpec(memory_space=pltpu.VMEM)
+    return pl.pallas_call(
+        results,
+        out_shape=(gradient, gradient, gradient, jax.ShapeDtypeStruct((piece, width * 8), F32)),
+        in_specs=[any_spec] * 3 + [vmem],
+        out_specs=(any_spec, any_spec, any_spec, vmem),
+        scratch_shapes=[pltpu.VMEM((3, rows, width * 8), BF16), dma((3,)), dma((3,))],
+        name="results",
+    )(*gradients, land)
+
+
+def results(dq_in, dk_in, dv_in, land, dq, dk, dv, gp, held, in_sem, out_sem):
+    ins, outs = (dq_in, dk_in, dv_in), (dq, dk, dv)
+    load = [pltpu.make_async_copy(ins[j], held.at[j], in_sem.at[j]) for j in range(3)]
+    store = [pltpu.make_async_copy(held.at[j], outs[j], out_sem.at[j]) for j in range(3)]
+    for copy in load:
+        copy.start()
+    for j in range(3):
+        load[j].wait()
+        store[j].start()
+    width = land.shape[2]
+    for source in range(8):
+        gp[:, source * width : (source + 1) * width] = land[source].astype(F32)
+    for copy in store:
+        copy.wait()
 
 
 def solution(mesh):

time: 177 us -> 159 us (0.90)
  the two profiles are of different devices: /device:TPU:1 before, /device:TPU:3 now
where the time goes in v3:
time: 159 us
  Pallas kernels  158 us (99%)
    pallas_call x1, Pallas kernels, local(): pl.pallas_call(functools.partial(kernel, dims), out_shape=(gradient, grad...  154 us
    pallas_call x1, Pallas kernels, local(): pl.pallas_call(results, out_shape=(gradient, gradient, gradient, jax.Shap...  4.11 us

profile of v3, /device:TPU:3, one launch (start us, length us, event | category | flops | bytes accessed | tf_op | source)
XLA Modules:
  0.0 158.7 jit_solution(3308317634192204555)
XLA Ops:
  0.6 154.0 %group_backward.1 = (bf16[128,2048]{1,0:T(8,128)(2,1)}, bf16[128,2048]{1,0:T(8,128)(2,1)}, bf16[128,2048]{1,0:T(8,128)(2,1)}, bf16[8,96,256]{2,1,0:T(8,128)(2,1)}) custom-call(s32[1,4]{1,0:T(1,128)} %counts.1, s32[1,16]{1,0:T(1,128)} %slots.1, bf16[128,3072]{1,0:T(8,128)(2,1)} %g_in.1, bf16[128,2048]{1,0:T(8,128)(2,1)} %q_in.1, bf16[128,2048]{1,0:T(8,128)(2,1)} %k_in.1, ...), custom_call_target="tpu_custom_call" | custom-call | tf_op jit(solution)/shard_map/group_backward/pallas_call | solution.py:445
  154.6 4.1 %results.1 = (bf16[128,2048]{1,0:T(8,128)(2,1)}, bf16[128,2048]{1,0:T(8,128)(2,1)}, bf16[128,2048]{1,0:T(8,128)(2,1)}, f32[96,2048]{1,0:T(8,128)}) custom-call(bf16[128,2048]{1,0:T(8,128)(2,1)} %get-tuple-element.8.dq_in, bf16[128,2048]{1,0:T(8,128)(2,1)} %get-tuple-element.9.dk_in, bf16[128,2048]{1,0:T(8,128)(2,1)} %get-tuple-element.10.dv_in, ...), custom_call_target="tpu_custom_call" | custom-call | tf_op jit(solution)/shard_map/results/pallas_call | solution.py:491

commit v4 on v3

v4 whole, which is shorter than its diff:
```python
import functools
import math

import jax
import jax.numpy as jnp
from jax import lax
from jax.experimental import pallas as pl
from jax.experimental.pallas import tpu as pltpu
from jax.sharding import PartitionSpec as P

HEAD_DIM = 128
VIEW_TOK = 64
HEADS_HERE = 2
CHIPS = 4
BF16 = jnp.bfloat16
F32 = jnp.float32
MESH = pl.DeviceIdType.MESH


def dot(a, b, contract):
    return lax.dot_general(a, b, ((contract[:1], contract[1:]), ((), ())), preferred_element_type=F32)


def kernel(
    dims,
    counts,
    slots,
    g_in,
    q_in,
    k_in,
    v_in,
    w_in,
    dq_out,
    dk_out,
    dv_out,
    land_out,
    g_chip,
    w_all,
    qkv,
    probs,
    att,
    att_send,
    att_recv,
    go_send,
    go_all,
    dk_acc,
    dv_acc,
    d_send,
    gp_send,
    first_recv,
    second_send,
    second_recv,
    gp_sum,
    line_send,
    line_recv,
    gp_last,
    slot_obj,
    key_obj,
    w_local_sem,
    w_pair_sem,
    w_one_send,
    w_one_recv,
    w_two_send,
    w_two_recv,
    g_local_sem,
    g_sem,
    qkv_recv_sem,
    qkv_send_sem,
    att_send_sem,
    att_recv_sem,
    go_send_sem,
    go_recv_sem,
    d_recv_sem,
    d_send_sem,
    first_send_sem,
    first_recv_sem,
    second_send_sem,
    second_recv_sem,
    line_send_sem,
    line_recv_sem,
    land_send_sem,
    land_recv_sem,
):
    side, rows, width, piece = dims
    chip_rows = 2 * rows
    tokens = 8 * rows
    model = side * side * 2 * piece
    scale = 1.0 / math.sqrt(HEAD_DIM)
    dp = lax.axis_index("dp")
    cam = lax.axis_index("cam")
    spot, z_lo = dp // 2, dp % 2
    y, x = spot // side, spot % side
    pair = spot * 2 + (1 - z_lo)
    chip, core = cam // 2, cam % 2
    sibling = chip * 2 + (1 - core)
    outs = (dq_out, dk_out, dv_out)
    ins = (q_in, k_in, v_in)

    def block(index):
        return pl.ds(pl.multiple_of(index * rows, rows), rows)

    def chip_block(index):
        return pl.ds(pl.multiple_of(index * chip_rows, chip_rows), chip_rows)

    def cols(index):
        return pl.ds(pl.multiple_of(index * width, width), width)

    def half_piece(index):
        return pl.ds(pl.multiple_of(index * piece, piece), piece)

    def remote(src, dst, send, recv, **where):
        return pltpu.make_async_remote_copy(
            src_ref=src, dst_ref=dst, send_sem=send, recv_sem=recv, device_id=where, device_id_type=MESH
        )

    def arrived(ref, sem):
        pltpu.make_async_copy(ref, ref, sem).wait()

    def at_x(c):
        return (y * side + c) * 2 + z_lo

    def at_y(c):
        return (c * side + x) * 2 + z_lo

    def mine(axis):
        return x if axis == "x" else y

    def other(axis, step):
        return (mine(axis) + step) % side

    def peer(axis, c):
        return at_x(c) if axis == "x" else at_y(c)

    gather_axes = (("y", "x"), ("x", "y"))
    reduce_axes = (("x", "y"), ("y", "x"))

    barrier = pltpu.get_barrier_semaphore()

    def greet(**where):
        pl.semaphore_signal(barrier, inc=1, device_id=where, device_id_type=MESH)

    for step in range(1, side):
        greet(dp=peer("x", other("x", step)))
        greet(dp=peer("y", other("y", step)))
    greet(dp=pair)
    for step in range(1, CHIPS):
        greet(dp=pair, cam=(chip + step) % CHIPS * 2 + core)

    @pl.loop(1, 8)
    def _(step):
        greet(cam=(cam + step) % 8)

    def w_local(c):
        return pltpu.make_async_copy(
            w_in.at[:, cols(c * 2 + core)], w_all.at[c, y, x, half_piece(z_lo), :], w_local_sem.at[c]
        )

    for c in range(CHIPS):
        w_local(c).start()

    def g_local():
        return pltpu.make_async_copy(g_in, g_chip.at[block(core), :], g_local_sem)

    g_local().start()
    pl.semaphore_wait(barrier, 2 * (side - 1) + 1 + (CHIPS - 1) + 7)

    def w_pair(z):
        here = w_all.at[:, y, x, half_piece(z), :]
        return remote(here, here, w_pair_sem.at[0], w_pair_sem.at[1], dp=pair)

    def w_one_ref(half, z, c):
        axis = gather_axes[half][0]
        at = (c, x) if axis == "y" else (y, c)
        return w_all.at[2 * half : 2 * half + 2, at[0], at[1], half_piece(z), :]

    def w_one(half, z, step):
        axis = gather_axes[half][0]
        here = w_one_ref(half, z, mine(axis))
        return remote(
            here,
            here,
            w_one_send.at[half, z, step],
            w_one_recv.at[half, z, mine(axis)],
            dp=peer(axis, other(axis, step)),
        )

    def w_two_ref(half, c):
        if gather_axes[half][1] == "x":
            return w_all.at[2 * half : 2 * half + 2, :, c, :, :]
        return w_all.at[2 * half : 2 * half + 2, c, :, :, :]

    def w_two(half, step):
        axis = gather_axes[half][1]
        here = w_two_ref(half, mine(axis))
        return remote(
            here,
            here,
            w_two_send.at[half, step],
            w_two_recv.at[half, mine(axis)],
            dp=peer(axis, other(axis, step)),
        )

    for c in range(CHIPS):
        w_local(c).wait()
    w_pair(z_lo).start()
    for half in range(2):
        for step in range(1, side):
            w_one(half, z_lo, step).start()

    def qkv_copy(j, step):
        target = (cam + step) % 8
        return remote(
            ins[j].at[:, cols(target)],
            qkv.at[j, block(cam), :],
            qkv_send_sem.at[step, j],
            qkv_recv_sem.at[cam, j],
            cam=target,
        )

    for j in range(3):

        @pl.loop(1, 8)
        def _(step):
            qkv_copy(j, step).start()

        pltpu.make_async_copy(
            ins[j].at[:, cols(cam)], qkv.at[j, block(cam), :], qkv_recv_sem.at[cam, j]
        ).start()

    g_copy = remote(g_in, g_chip.at[block(core), :], g_sem.at[0], g_sem.at[1], cam=sibling)
    g_copy.start()

    arrived(w_all.at[:, y, x, half_piece(1 - z_lo), :], w_pair_sem.at[1])
    for half in range(2):
        for step in range(1, side):
            w_one(half, 1 - z_lo, step).start()

    ends = [counts[0, 0]]
    for o in range(1, counts.shape[1]):
        ends.append(ends[-1] + counts[0, o])
    views = slots.shape[1]
    view_obj = [sum((v >= end).astype(jnp.int32) for end in ends) for v in range(views)]

    @pl.loop(0, views)
    def _(s):
        found = jnp.int32(0)
        for v in range(views):
            found = found + jnp.where(slots[0, v] == s, view_obj[v], 0)
        slot_obj[s] = found

    lane_slot = lax.broadcasted_iota(jnp.int32, (1, tokens), 1) // VIEW_TOK
    lane_obj = jnp.zeros((1, tokens), jnp.int32)
    for s in range(views):
        lane_obj = jnp.where(lane_slot == s, slot_obj[s], lane_obj)
    key_obj[...] = lane_obj
    dk_acc[...] = jnp.zeros_like(dk_acc)
    dv_acc[...] = jnp.zeros_like(dv_acc)

    for half in range(2):
        axis = gather_axes[half][0]
        for step in range(1, side):
            for z in range(2):
                c = other(axis, step)
                arrived(w_one_ref(half, z, c), w_one_recv.at[half, z, c])
    for half in range(2):
        for step in range(1, side):
            w_two(half, step).start()

    for j in range(3):

        @pl.loop(0, 8)
        def _(source):
            arrived(qkv.at[j, block(source), :], qkv_recv_sem.at[source, j])

    def att_copy(c):
        return remote(
            att_send.at[chip_block(c), :],
            att_recv.at[:, cols(chip)],
            att_send_sem.at[c],
            att_recv_sem.at[chip],
            cam=c * 2 + core,
        )

    def nth(u, first, second, third, fourth):
        return jnp.where(u == 0, first, jnp.where(u == 1, second, jnp.where(u == 2, third, fourth)))

    @pl.loop(0, CHIPS)
    def _(u):
        c = (chip + nth(u, 2, 1, 3, 0)) % CHIPS

        @pl.loop(0, 2)
        def _(k):
            r = c * 2 + k
            here = block(r)
            row = lax.broadcasted_iota(jnp.int32, (rows, 1), 0)
            row_obj = jnp.where(row < VIEW_TOK, slot_obj[r * 2], slot_obj[r * 2 + 1])
            same = row_obj == key_obj[...]
            for i in range(HEADS_HERE):
                head = slice(i * HEAD_DIM, (i + 1) * HEAD_DIM)
                scores = dot(qkv[0, here, head], qkv[1, :, head], (1, 1)) * scale
                scores = jnp.where(same, scores, -jnp.inf)
                exps = jnp.exp(scores - jnp.max(scores, axis=1, keepdims=True))
                p = exps * (1.0 / jnp.sum(exps, axis=1, keepdims=True))
                probs[i, here, :] = p
                att[here, head] = dot(p.astype(BF16), qkv[2, :, head], (1, 0))

        there = chip_block(c)

        @pl.when(u < CHIPS - 1)
        def _():
            att_send[there, :] = att[there, :].astype(BF16)
            att_copy(c).start()

        @pl.when(u == CHIPS - 1)
        def _():
            att_recv[:, cols(chip)] = att[there, :].astype(BF16)

    for half in range(2):
        axis = gather_axes[half][1]
        for step in range(1, side):
            c = other(axis, step)
            arrived(w_two_ref(half, c), w_two_recv.at[half, c])
    g_local().wait()
    arrived(g_chip.at[block(1 - core), :], g_sem.at[1])

    def go_copy(c):
        return remote(
            go_send.at[c], go_all.at[chip_block(chip), :], go_send_sem.at[c], go_recv_sem.at[chip], cam=c * 2 + core
        )

    @pl.loop(0, CHIPS)
    def _(u):
        c = (chip + nth(u, 2, 1, 3, 0)) % CHIPS
        grad_att = dot(g_chip[...], w_all[c].reshape(model, width), (1, 0)).astype(BF16)

        @pl.when(u < CHIPS - 1)
        def _():
            go_send[c] = grad_att
            go_copy(c).start()

        @pl.when(u == CHIPS - 1)
        def _():
            go_all[chip_block(chip), :] = grad_att

    for step in range(1, CHIPS):
        c = (chip + step) % CHIPS
        arrived(att_recv.at[:, cols(c)], att_recv_sem.at[c])

    def first_copy(half, step):
        axis = reduce_axes[half][0]
        c = other(axis, step)
        src = gp_send.at[2 * half : 2 * half + 2, :, c] if axis == "x" else gp_send.at[2 * half : 2 * half + 2, c]
        return remote(
            src,
            first_recv.at[half, mine(axis)],
            first_send_sem.at[half, step],
            first_recv_sem.at[half, mine(axis)],
            dp=peer(axis, c),
        )

    for half in range(2):
        att_half = att_recv[:, 2 * half * width : 2 * (half + 1) * width]

        @pl.loop(0, side * side // 2)
        def _(j):
            tile = pl.ds(pl.multiple_of(j * 4 * piece, 128), 4 * piece)
            total = dot(g_chip[:, tile], att_half, (0, 0)).astype(BF16)
            for s in range(2):
                for c in range(2):
                    gp_send[2 * half + c, (2 * j + s) // side, (2 * j + s) % side] = total[
                        s * 2 * piece : (s + 1) * 2 * piece, c * width : (c + 1) * width
                    ]

        for step in range(1, side):
            first_copy(half, step).start()

    def d_copy(j, target):
        return remote(
            d_send.at[j, block(target), :],
            outs[j].at[:, cols(cam)],
            d_send_sem.at[target, j],
            d_recv_sem.at[cam, j],
            cam=target,
        )

    def d_local(j):
        return pltpu.make_async_copy(
            d_send.at[j, block(cam), :], outs[j].at[:, cols(cam)], d_recv_sem.at[cam, j]
        )

    @pl.loop(0, CHIPS)
    def _(t):
        c = (chip + nth(t, 0, 3, 1, 2)) % CHIPS
        here = chip_block(c)

        @pl.when(t > 0)
        def _():
            arrived(go_all.at[here, :], go_recv_sem.at[c])

        for i in range(HEADS_HERE):
            head = slice(i * HEAD_DIM, (i + 1) * HEAD_DIM)
            go = go_all[here, head]
            p = probs[i, here, :]
            delta = jnp.sum(go.astype(F32) * att[here, head], axis=1, keepdims=True)
            ds = (p * (dot(go, qkv[2, :, head], (1, 1)) - delta)).astype(BF16)
            d_send[0, here, head] = (dot(ds, qkv[1, :, head], (1, 0)) * scale).astype(BF16)
            dk_acc[:, head] += dot(ds, qkv[0, here, head], (0, 0))
            dv_acc[:, head] += dot(p.astype(BF16), go, (0, 0))

        @pl.when(t == 0)
        def _():
            d_local(0).start()
            d_copy(0, sibling).start()

        @pl.when(t > 0)
        def _():
            d_copy(0, c * 2).start()
            d_copy(0, c * 2 + 1).start()

    d_send[1] = (dk_acc[...] * scale).astype(BF16)
    d_send[2] = dv_acc[...].astype(BF16)
    for j in range(1, 3):

        @pl.loop(1, 8)
        def _(step):
            d_copy(j, (cam + step) % 8).start()

        d_local(j).start()

    def second_copy(half, step):
        axis = reduce_axes[half][1]
        c = other(axis, step)
        return remote(
            second_send.at[half, c],
            second_recv.at[half, mine(axis)],
            second_send_sem.at[half, step],
            second_recv_sem.at[half, mine(axis)],
            dp=peer(axis, c),
        )

    for half in range(2):
        axis, later = reduce_axes[half]
        for step in range(1, side):
            c = other(axis, step)
            arrived(first_recv.at[half, c], first_recv_sem.at[half, c])

        def partial(i):
            own = (slice(2 * half, 2 * half + 2), i, x) if axis == "x" else (slice(2 * half, 2 * half + 2), y, i)
            total = gp_send[own].astype(F32)
            for step in range(1, side):
                total = total + first_recv[half, other(axis, step), :, i].astype(F32)
            return total

        for step in range(1, side):
            i = other(later, step)
            second_send[half, i] = partial(i).astype(BF16)
            second_copy(half, step).start()
        gp_sum[2 * half : 2 * half + 2] = partial(mine(later))

    for half in range(2):
        later = reduce_axes[half][1]
        for step in range(1, side):
            c = other(later, step)
            arrived(second_recv.at[half, c], second_recv_sem.at[half, c])
            gp_sum[2 * half : 2 * half + 2] += second_recv[half, c].astype(F32)

    line_send[...] = gp_sum[...].astype(BF16)
    here_z = chip * 2 + z_lo

    def line_copy(step):
        target = (here_z + step) % 8
        return remote(
            line_send.at[target // 2, half_piece(target % 2), :],
            line_recv.at[here_z],
            line_send_sem.at[step],
            line_recv_sem.at[here_z],
            dp=spot * 2 + target % 2,
            cam=target // 2 * 2 + core,
        )

    @pl.loop(1, 8)
    def _(step):
        line_copy(step).start()

    total = gp_sum[chip, half_piece(z_lo), :]
    for step in range(1, 8):
        source = (here_z + 8 - step) % 8
        arrived(line_recv.at[source], line_recv_sem.at[source])
        total = total + line_recv[source].astype(F32)
    gp_last[...] = total.astype(BF16)

    def land_copy(step):
        return remote(
            gp_last, land_out.at[cam], land_send_sem.at[step], land_recv_sem.at[cam], cam=(cam + step) % 8
        )

    pltpu.make_async_copy(gp_last, land_out.at[cam], land_recv_sem.at[cam]).start()

    @pl.loop(1, 8)
    def _(step):
        land_copy(step).start()

    for j in range(3):

        @pl.loop(0, 8)
        def _(source):
            arrived(outs[j].at[:, cols(source)], d_recv_sem.at[source, j])

    @pl.loop(0, 8)
    def _(source):
        arrived(land_out.at[source], land_recv_sem.at[source])

    w_pair(z_lo).wait_send()
    g_copy.wait_send()
    for half in range(2):
        for step in range(1, side):
            for z in range(2):
                w_one(half, z, step).wait_send()
            w_two(half, step).wait_send()
            first_copy(half, step).wait_send()
            second_copy(half, step).wait_send()
    for step in range(1, CHIPS):
        c = (chip + step) % CHIPS
        att_copy(c).wait_send()
        go_copy(c).wait_send()

    @pl.loop(1, 8)
    def _(step):
        for j in range(3):
            qkv_copy(j, step).wait_send()
            d_copy(j, (cam + step) % 8).wait_send()
        line_copy(step).wait_send()
        land_copy(step).wait_send()


def local(grad_out, query_act, key_act, value_act, out_proj, view_counts, view_slots):
    rows, model = grad_out.shape
    planes = lax.axis_size("dp") // 2
    side = math.isqrt(planes)
    piece = out_proj.shape[0]
    width = query_act.shape[1] // 8
    tokens = rows * 8
    dims = (side, rows, width, piece)
    any_spec = pl.BlockSpec(memory_space=pl.ANY)
    dma = pltpu.SemaphoreType.DMA
    gradient = jax.ShapeDtypeStruct(query_act.shape, BF16)
    *gradients, land = pl.pallas_call(
        functools.partial(kernel, dims),
        out_shape=(gradient, gradient, gradient, jax.ShapeDtypeStruct((8, piece, width), BF16)),
        in_specs=[pl.BlockSpec(memory_space=pltpu.SMEM)] * 2 + [any_spec] * 5,
        out_specs=(any_spec,) * 4,
        scratch_shapes=[
            pltpu.VMEM((2 * rows, model), BF16),
            pltpu.VMEM((CHIPS, side, side, 2 * piece, width), BF16),
            pltpu.VMEM((3, tokens, width), BF16),
            pltpu.VMEM((HEADS_HERE, tokens, tokens), F32),
            pltpu.VMEM((tokens, width), F32),
            pltpu.VMEM((tokens, width), BF16),
            pltpu.VMEM((2 * rows, CHIPS * width), BF16),
            pltpu.VMEM((CHIPS, 2 * rows, width), BF16),
            pltpu.VMEM((tokens, width), BF16),
            pltpu.VMEM((tokens, width), F32),
            pltpu.VMEM((tokens, width), F32),
            pltpu.VMEM((3, tokens, width), BF16),
            pltpu.VMEM((CHIPS, side, side, 2 * piece, width), BF16),
            pltpu.VMEM((2, side, 2, side, 2 * piece, width), BF16),
            pltpu.VMEM((2, side, 2, 2 * piece, width), BF16),
            pltpu.VMEM((2, side, 2, 2 * piece, width), BF16),
            pltpu.VMEM((CHIPS, 2 * piece, width), F32),
            pltpu.VMEM((CHIPS, 2 * piece, width), BF16),
            pltpu.VMEM((8, piece, width), BF16),
            pltpu.VMEM((piece, width), BF16),
            pltpu.SMEM((view_slots.shape[1],), jnp.int32),
            pltpu.VMEM((1, tokens), jnp.int32),
            dma((CHIPS,)),
            dma((2,)),
            dma((2, 2, side)),
            dma((2, 2, side)),
            dma((2, side)),
            dma((2, side)),
            dma,
            dma((2,)),
            dma((8, 3)),
            dma((8, 3)),
            dma((CHIPS,)),
            dma((CHIPS,)),
            dma((CHIPS,)),
            dma((CHIPS,)),
            dma((8, 3)),
            dma((8, 3)),
            dma((2, side)),
            dma((2, side)),
            dma((2, side)),
            dma((2, side)),
            dma((8,)),
            dma((8,)),
            dma((8,)),
            dma((8,)),
        ],
        compiler_params=pltpu.CompilerParams(
            collective_id=0, has_side_effects=True, vmem_limit_bytes=60 * 1024 * 1024
        ),
        name="group_backward",
    )(view_counts, view_slots, grad_out, query_act, key_act, value_act, out_proj)
    vmem = pl.BlockSpec(memory_space=pltpu.VMEM)
    return pl.pallas_call(
        results,
        out_shape=(gradient, gradient, gradient, jax.ShapeDtypeStruct((piece, width * 8), F32)),
        in_specs=[any_spec] * 3 + [vmem],
        out_specs=(any_spec, any_spec, any_spec, vmem),
        scratch_shapes=[pltpu.VMEM((3, rows, width * 8), BF16), dma((3,)), dma((3,))],
        name="results",
    )(*gradients, land)


def results(dq_in, dk_in, dv_in, land, dq, dk, dv, gp, held, in_sem, out_sem):
    ins, outs = (dq_in, dk_in, dv_in), (dq, dk, dv)
    load = [pltpu.make_async_copy(ins[j], held.at[j], in_sem.at[j]) for j in range(3)]
    store = [pltpu.make_async_copy(held.at[j], outs[j], out_sem.at[j]) for j in range(3)]
    for copy in load:
        copy.start()
    for j in range(3):
        load[j].wait()
        store[j].start()
    width = land.shape[2]
    for source in range(8):
        gp[:, source * width : (source + 1) * width] = land[source].astype(F32)
    for copy in store:
        copy.wait()


def solution(mesh):
    rows = P(("dp", "cam"), None)
    in_specs = (rows, rows, rows, rows, P("dp", None), P("dp", None), P("dp", None))
    out_specs = (rows, rows, rows, P("dp", None))
    return jax.shard_map(local, mesh=mesh, in_specs=in_specs, out_specs=out_specs, check_vma=False)
```

time: 159 us -> 150 us (0.943)
  the two profiles are of different devices: /device:TPU:3 before, /device:TPU:1 now
where the time goes in v4:
time: 150 us
  Pallas kernels  149 us (99%)
    pallas_call x1, Pallas kernels, local(): pl.pallas_call(functools.partial(kernel, dims), out_shape=(gradient, grad...  145 us
    pallas_call x1, Pallas kernels, local(): pl.pallas_call(results, out_shape=(gradient, gradient, gradient, jax.Shap...  4.11 us

profile of v4, /device:TPU:1, one launch (start us, length us, event | category | flops | bytes accessed | tf_op | source)
XLA Modules:
  0.0 150.0 jit_solution(511269400514483166)
XLA Ops:
  0.6 145.3 %group_backward.1 = (bf16[128,2048]{1,0:T(8,128)(2,1)}, bf16[128,2048]{1,0:T(8,128)(2,1)}, bf16[128,2048]{1,0:T(8,128)(2,1)}, bf16[8,96,256]{2,1,0:T(8,128)(2,1)}) custom-call(s32[1,4]{1,0:T(1,128)} %counts.1, s32[1,16]{1,0:T(1,128)} %slots.1, bf16[128,3072]{1,0:T(8,128)(2,1)} %g_in.1, bf16[128,2048]{1,0:T(8,128)(2,1)} %q_in.1, bf16[128,2048]{1,0:T(8,128)(2,1)} %k_in.1, ...), custom_call_target="tpu_custom_call" | custom-call | tf_op jit(solution)/shard_map/group_backward/pallas_call | solution.py:547
  145.9 4.1 %results.1 = (bf16[128,2048]{1,0:T(8,128)(2,1)}, bf16[128,2048]{1,0:T(8,128)(2,1)}, bf16[128,2048]{1,0:T(8,128)(2,1)}, f32[96,2048]{1,0:T(8,128)}) custom-call(bf16[128,2048]{1,0:T(8,128)(2,1)} %get-tuple-element.8.dq_in, bf16[128,2048]{1,0:T(8,128)(2,1)} %get-tuple-element.9.dk_in, bf16[128,2048]{1,0:T(8,128)(2,1)} %get-tuple-element.10.dv_in, ...), custom_call_target="tpu_custom_call" | custom-call | tf_op jit(solution)/shard_map/results/pallas_call | solution.py:606

commit v5 on v4

--- a/solution.py
+++ b/solution.py
@@ -47,6 +47,7 @@
     dv_acc,
     d_send,
     gp_send,
+    far_recv,
     first_recv,
     second_send,
     second_recv,
@@ -61,6 +62,7 @@
     w_one_send,
     w_one_recv,
     w_two_send,
+    w_pass_send,
     w_two_recv,
     g_local_sem,
     g_sem,
@@ -72,6 +74,8 @@
     go_recv_sem,
     d_recv_sem,
     d_send_sem,
+    far_send_sem,
+    far_recv_sem,
     first_send_sem,
     first_recv_sem,
     second_send_sem,
@@ -164,9 +168,15 @@
     g_local().start()
     pl.semaphore_wait(barrier, 2 * (side - 1) + 1 + (CHIPS - 1) + 7)
 
-    def w_pair(z):
-        here = w_all.at[:, y, x, half_piece(z), :]
-        return remote(here, here, w_pair_sem.at[0], w_pair_sem.at[1], dp=pair)
+    def w_pair_ref(half, z):
+        return w_all.at[2 * half : 2 * half + 2, y, x, half_piece(z), :]
+
+    def w_pair(half):
+        here = w_pair_ref(half, z_lo)
+        there = (chip + half * (CHIPS - 1 + 2 * z_lo)) % CHIPS
+        return remote(
+            here, here, w_pair_sem.at[0, half], w_pair_sem.at[1, half], dp=pair, cam=there * 2 + core
+        )
 
     def w_one_ref(half, z, c):
         axis = gather_axes[half][0]
@@ -184,25 +194,43 @@
             dp=peer(axis, other(axis, step)),
         )
 
-    def w_two_ref(half, c):
+    def w_two_ref(half, z, c):
         if gather_axes[half][1] == "x":
-            return w_all.at[2 * half : 2 * half + 2, :, c, :, :]
-        return w_all.at[2 * half : 2 * half + 2, c, :, :, :]
-
-    def w_two(half, step):
+            return w_all.at[2 * half : 2 * half + 2, :, c, half_piece(z), :]
+        return w_all.at[2 * half : 2 * half + 2, c, :, half_piece(z), :]
+
+    def w_two(half, z, way):
         axis = gather_axes[half][1]
-        here = w_two_ref(half, mine(axis))
+        here = w_two_ref(half, z, mine(axis))
         return remote(
             here,
             here,
-            w_two_send.at[half, step],
-            w_two_recv.at[half, mine(axis)],
-            dp=peer(axis, other(axis, step)),
-        )
+            w_two_send.at[half, z, way],
+            w_two_recv.at[half, z, mine(axis)],
+            dp=peer(axis, other(axis, 1 if way == 0 else side - 1)),
+        )
+
+    def w_from(half, z):
+        return other(gather_axes[half][1], side - 1 + 2 * z)
+
+    def w_pass(half, z):
+        axis = gather_axes[half][1]
+        here = w_two_ref(half, z, w_from(half, z))
+        return remote(
+            here,
+            here,
+            w_pass_send.at[half, z],
+            w_two_recv.at[half, z, w_from(half, z)],
+            dp=peer(axis, other(axis, side + 1 - 2 * z)),
+        )
+
+    def w_two_wait(half, z, c):
+        arrived(w_two_ref(half, z, c), w_two_recv.at[half, z, c])
 
     for c in range(CHIPS):
         w_local(c).wait()
-    w_pair(z_lo).start()
+    for half in range(2):
+        w_pair(half).start()
     for half in range(2):
         for step in range(1, side):
             w_one(half, z_lo, step).start()
@@ -217,8 +245,7 @@
             cam=target,
         )
 
-    for j in range(3):
-
+    def qkv_start(j):
         @pl.loop(1, 8)
         def _(step):
             qkv_copy(j, step).start()
@@ -227,13 +254,16 @@
             ins[j].at[:, cols(cam)], qkv.at[j, block(cam), :], qkv_recv_sem.at[cam, j]
         ).start()
 
+    qkv_start(0)
+
     g_copy = remote(g_in, g_chip.at[block(core), :], g_sem.at[0], g_sem.at[1], cam=sibling)
     g_copy.start()
 
-    arrived(w_all.at[:, y, x, half_piece(1 - z_lo), :], w_pair_sem.at[1])
-    for half in range(2):
+    for half in range(2):
+        arrived(w_pair_ref(half, 1 - z_lo), w_pair_sem.at[1, half])
         for step in range(1, side):
             w_one(half, 1 - z_lo, step).start()
+    qkv_start(1)
 
     ends = [counts[0, 0]]
     for o in range(1, counts.shape[1]):
@@ -256,16 +286,16 @@
     dk_acc[...] = jnp.zeros_like(dk_acc)
     dv_acc[...] = jnp.zeros_like(dv_acc)
 
-    for half in range(2):
-        axis = gather_axes[half][0]
-        for step in range(1, side):
-            for z in range(2):
+    for z in (z_lo, 1 - z_lo):
+        for half in range(2):
+            axis = gather_axes[half][0]
+            for step in range(1, side):
                 c = other(axis, step)
                 arrived(w_one_ref(half, z, c), w_one_recv.at[half, z, c])
-    for half in range(2):
-        for step in range(1, side):
-            w_two(half, step).start()
-
+            for way in range(2):
+                w_two(half, z, way).start()
+        if z is z_lo:
+            qkv_start(2)
     for j in range(3):
 
         @pl.loop(0, 8)
@@ -306,6 +336,13 @@
 
         there = chip_block(c)
 
+        @pl.when(u < 2)
+        def _():
+            z = jnp.where(u == 0, z_lo, 1 - z_lo)
+            for half in range(2):
+                w_two_wait(half, z, w_from(half, z))
+                w_pass(half, z).start()
+
         @pl.when(u < CHIPS - 1)
         def _():
             att_send[there, :] = att[there, :].astype(BF16)
@@ -315,47 +352,38 @@
         def _():
             att_recv[:, cols(chip)] = att[there, :].astype(BF16)
 
-    for half in range(2):
-        axis = gather_axes[half][1]
-        for step in range(1, side):
-            c = other(axis, step)
-            arrived(w_two_ref(half, c), w_two_recv.at[half, c])
     g_local().wait()
     arrived(g_chip.at[block(1 - core), :], g_sem.at[1])
-
-    def go_copy(c):
-        return remote(
-            go_send.at[c], go_all.at[chip_block(chip), :], go_send_sem.at[c], go_recv_sem.at[chip], cam=c * 2 + core
-        )
-
-    @pl.loop(0, CHIPS)
-    def _(u):
-        c = (chip + nth(u, 2, 1, 3, 0)) % CHIPS
-        grad_att = dot(g_chip[...], w_all[c].reshape(model, width), (1, 0)).astype(BF16)
-
-        @pl.when(u < CHIPS - 1)
-        def _():
-            go_send[c] = grad_att
-            go_copy(c).start()
-
-        @pl.when(u == CHIPS - 1)
-        def _():
-            go_all[chip_block(chip), :] = grad_att
 
     for step in range(1, CHIPS):
         c = (chip + step) % CHIPS
         arrived(att_recv.at[:, cols(c)], att_recv_sem.at[c])
 
-    def first_copy(half, step):
+    def first_part(half, part, c):
+        if reduce_axes[half][0] == "x":
+            return gp_send.at[2 * half + part, :, c]
+        return gp_send.at[2 * half + part, c]
+
+    def toward(half, part):
+        return other(reduce_axes[half][0], 1 if part == 0 else side - 1)
+
+    def far_copy(half, part):
         axis = reduce_axes[half][0]
-        c = other(axis, step)
-        src = gp_send.at[2 * half : 2 * half + 2, :, c] if axis == "x" else gp_send.at[2 * half : 2 * half + 2, c]
-        return remote(
-            src,
-            first_recv.at[half, mine(axis)],
-            first_send_sem.at[half, step],
-            first_recv_sem.at[half, mine(axis)],
-            dp=peer(axis, c),
+        return remote(
+            first_part(half, part, other(axis, 2)),
+            far_recv.at[half, part],
+            far_send_sem.at[half, part],
+            far_recv_sem.at[half, part],
+            dp=peer(axis, toward(half, part)),
+        )
+
+    def first_copy(half, way, part):
+        return remote(
+            first_part(half, part, toward(half, way)),
+            first_recv.at[half, way, part],
+            first_send_sem.at[half, way, part],
+            first_recv_sem.at[half, way, part],
+            dp=peer(reduce_axes[half][0], toward(half, way)),
         )
 
     for half in range(2):
@@ -371,8 +399,37 @@
                         s * 2 * piece : (s + 1) * 2 * piece, c * width : (c + 1) * width
                     ]
 
-        for step in range(1, side):
-            first_copy(half, step).start()
+        for part in range(2):
+            far_copy(half, part).start()
+
+    for half in range(2):
+        axis = gather_axes[half][1]
+        for z in range(2):
+            w_two_wait(half, z, other(axis, 1 + (side - 2) * z))
+            for step in range(2, side - 1):
+                w_two_wait(half, z, other(axis, step))
+    def go_copy(c):
+        return remote(
+            go_send.at[c], go_all.at[chip_block(chip), :], go_send_sem.at[c], go_recv_sem.at[chip], cam=c * 2 + core
+        )
+
+    @pl.loop(0, CHIPS)
+    def _(u):
+        c = (chip + nth(u, 2, 1, 3, 0)) % CHIPS
+        grad_att = dot(g_chip[...], w_all[c].reshape(model, width), (1, 0)).astype(BF16)
+
+        @pl.when(u < CHIPS - 1)
+        def _():
+            go_send[c] = grad_att
+            go_copy(c).start()
+
+        @pl.when(u == CHIPS - 1)
+        def _():
+            go_all[chip_block(chip), :] = grad_att
+
+    for half in range(2):
+        for part in range(2):
+            first_copy(half, 1 - part, part).start()
 
     def d_copy(j, target):
         return remote(
@@ -396,6 +453,15 @@
         @pl.when(t > 0)
         def _():
             arrived(go_all.at[here, :], go_recv_sem.at[c])
+
+        @pl.when(t == 2)
+        def _():
+            for half in range(2):
+                for part in range(2):
+                    arrived(far_recv.at[half, part], far_recv_sem.at[half, part])
+                    own = first_part(half, part, toward(half, part))
+                    own[...] = (own[...].astype(F32) + far_recv[half, part].astype(F32)).astype(BF16)
+                    first_copy(half, part, part).start()
 
         for i in range(HEADS_HERE):
             head = slice(i * HEAD_DIM, (i + 1) * HEAD_DIM)
@@ -440,15 +506,15 @@
 
     for half in range(2):
         axis, later = reduce_axes[half]
-        for step in range(1, side):
-            c = other(axis, step)
-            arrived(first_recv.at[half, c], first_recv_sem.at[half, c])
+        for way in range(2):
+            for part in range(2):
+                arrived(first_recv.at[half, way, part], first_recv_sem.at[half, way, part])
 
         def partial(i):
             own = (slice(2 * half, 2 * half + 2), i, x) if axis == "x" else (slice(2 * half, 2 * half + 2), y, i)
             total = gp_send[own].astype(F32)
-            for step in range(1, side):
-                total = total + first_recv[half, other(axis, step), :, i].astype(F32)
+            for way in range(2):
+                total = total + first_recv[half, way, :, i].astype(F32)
             return total
 
         for step in range(1, side):
@@ -490,15 +556,21 @@
     gp_last[...] = total.astype(BF16)
 
     def land_copy(step):
-        return remote(
-            gp_last, land_out.at[cam], land_send_sem.at[step], land_recv_sem.at[cam], cam=(cam + step) % 8
-        )
-
+        target = (chip + step) % CHIPS * 2 + core if step else sibling
+        return remote(gp_last, land_out.at[cam], land_send_sem.at[step], land_recv_sem.at[cam], cam=target)
+
+    def land_pass(step):
+        source = (chip + step) % CHIPS * 2 + core
+        here = land_out.at[source]
+        return remote(here, here, land_send_sem.at[CHIPS + step], land_recv_sem.at[source], cam=sibling)
+
+    for step in (2, 1, 3, 0):
+        land_copy(step).start()
     pltpu.make_async_copy(gp_last, land_out.at[cam], land_recv_sem.at[cam]).start()
-
-    @pl.loop(1, 8)
-    def _(step):
-        land_copy(step).start()
+    for step in (1, 3, 2):
+        source = (chip + step) % CHIPS * 2 + core
+        arrived(land_out.at[source], land_recv_sem.at[source])
+        land_pass(step).start()
 
     for j in range(3):
 
@@ -506,19 +578,26 @@
         def _(source):
             arrived(outs[j].at[:, cols(source)], d_recv_sem.at[source, j])
 
-    @pl.loop(0, 8)
-    def _(source):
+    arrived(land_out.at[cam], land_recv_sem.at[cam])
+    for step in range(CHIPS):
+        source = (chip + step) % CHIPS * 2 + 1 - core
         arrived(land_out.at[source], land_recv_sem.at[source])
 
-    w_pair(z_lo).wait_send()
+    for half in range(2):
+        w_pair(half).wait_send()
     g_copy.wait_send()
     for half in range(2):
         for step in range(1, side):
             for z in range(2):
                 w_one(half, z, step).wait_send()
-            w_two(half, step).wait_send()
-            first_copy(half, step).wait_send()
             second_copy(half, step).wait_send()
+        for z in range(2):
+            w_pass(half, z).wait_send()
+            far_copy(half, z).wait_send()
+            for part in range(2):
+                first_copy(half, z, part).wait_send()
+            for way in range(2):
+                w_two(half, z, way).wait_send()
     for step in range(1, CHIPS):
         c = (chip + step) % CHIPS
         att_copy(c).wait_send()
@@ -530,7 +609,11 @@
             qkv_copy(j, step).wait_send()
             d_copy(j, (cam + step) % 8).wait_send()
         line_copy(step).wait_send()
+
+    for step in range(CHIPS):
         land_copy(step).wait_send()
+        if step:
+            land_pass(step).wait_send()
 
 
 def local(grad_out, query_act, key_act, value_act, out_proj, view_counts, view_slots):
@@ -563,7 +646,8 @@
             pltpu.VMEM((tokens, width), F32),
             pltpu.VMEM((3, tokens, width), BF16),
             pltpu.VMEM((CHIPS, side, side, 2 * piece, width), BF16),
-            pltpu.VMEM((2, side, 2, side, 2 * piece, width), BF16),
+            pltpu.VMEM((2, 2, side, 2 * piece, width), BF16),
+            pltpu.VMEM((2, 2, 2, side, 2 * piece, width), BF16),
             pltpu.VMEM((2, side, 2, 2 * piece, width), BF16),
             pltpu.VMEM((2, side, 2, 2 * piece, width), BF16),
             pltpu.VMEM((CHIPS, 2 * piece, width), F32),
@@ -573,11 +657,12 @@
             pltpu.SMEM((view_slots.shape[1],), jnp.int32),
             pltpu.VMEM((1, tokens), jnp.int32),
             dma((CHIPS,)),
-            dma((2,)),
+            dma((2, 2)),
             dma((2, 2, side)),
             dma((2, 2, side)),
-            dma((2, side)),
-            dma((2, side)),
+            dma((2, 2, 2)),
+            dma((2, 2)),
+            dma((2, 2, side)),
             dma,
             dma((2,)),
             dma((8, 3)),
@@ -588,8 +673,10 @@
             dma((CHIPS,)),
             dma((8, 3)),
             dma((8, 3)),
-            dma((2, side)),
-            dma((2, side)),
+            dma((2, 2)),
+            dma((2, 2)),
+            dma((2, 2, 2)),
+            dma((2, 2, 2)),
             dma((2, side)),
             dma((2, side)),
             dma((8,)),
@@ -602,29 +689,40 @@
         ),
         name="group_backward",
     )(view_counts, view_slots, grad_out, query_act, key_act, value_act, out_proj)
-    vmem = pl.BlockSpec(memory_space=pltpu.VMEM)
     return pl.pallas_call(
         results,
         out_shape=(gradient, gradient, gradient, jax.ShapeDtypeStruct((piece, width * 8), F32)),
-        in_specs=[any_spec] * 3 + [vmem],
-        out_specs=(any_spec, any_spec, any_spec, vmem),
-        scratch_shapes=[pltpu.VMEM((3, rows, width * 8), BF16), dma((3,)), dma((3,))],
+        in_specs=[any_spec] * 4,
+        out_specs=(any_spec,) * 4,
+        scratch_shapes=[
+            pltpu.VMEM((3, rows, width * 8), BF16),
+            pltpu.VMEM((8, piece, width), BF16),
+            pltpu.VMEM((piece, width * 8), F32),
+            dma((7,)),
+            dma((7,)),
+        ],
         name="results",
     )(*gradients, land)
 
 
-def results(dq_in, dk_in, dv_in, land, dq, dk, dv, gp, held, in_sem, out_sem):
-    ins, outs = (dq_in, dk_in, dv_in), (dq, dk, dv)
-    load = [pltpu.make_async_copy(ins[j], held.at[j], in_sem.at[j]) for j in range(3)]
-    store = [pltpu.make_async_copy(held.at[j], outs[j], out_sem.at[j]) for j in range(3)]
+def results(dq_in, dk_in, dv_in, land_in, dq, dk, dv, gp, held, land, wide, in_sem, out_sem):
+    half = dq.shape[0] // 2
+    load = [pltpu.make_async_copy(land_in, land, in_sem.at[6])]
+    store = [pltpu.make_async_copy(wide, gp, out_sem.at[6])]
+    for j, (a, b) in enumerate(((dq_in, dq), (dk_in, dk), (dv_in, dv))):
+        for k in range(2):
+            part = pl.ds(k * half, half)
+            load.append(pltpu.make_async_copy(a.at[part], held.at[j, part], in_sem.at[2 * j + k]))
+            store.append(pltpu.make_async_copy(held.at[j, part], b.at[part], out_sem.at[2 * j + k]))
     for copy in load:
         copy.start()
-    for j in range(3):
-        load[j].wait()
-        store[j].start()
     width = land.shape[2]
-    for source in range(8):
-        gp[:, source * width : (source + 1) * width] = land[source].astype(F32)
+    for index in (*range(1, 7), 0):
+        load[index].wait()
+        if index == 0:
+            for source in range(8):
+                wide[:, source * width : (source + 1) * width] = land[source].astype(F32)
+        store[index].start()
     for copy in store:
         copy.wait()
 

time: 150 us -> 143 us (0.953)
  Pallas kernels: 149 us -> 142 us
    pallas_call x1, Pallas kernels: 145 us -> 140 us  [local(): pl.pallas_call(functools.partial(kernel, dims), out_shape=(gradient, grad...]
    pallas_call x1, Pallas kernels: 4.11 us -> 2.6 us  [local(): pl.pallas_call(results, out_shape=(gradient, gradient, gradient, jax.Shap...]
where the time goes in v5:
time: 143 us
  Pallas kernels  142 us (99%)
    pallas_call x1, Pallas kernels, local(): pl.pallas_call(functools.partial(kernel, dims), out_shape=(gradient, grad...  140 us

profile of v5, /device:TPU:1, one launch (start us, length us, event | category | flops | bytes accessed | tf_op | source)
XLA Modules:
  0.0 143.0 jit_solution(12374367010322578132)
XLA Ops:
  0.6 139.8 %group_backward.1 = (bf16[128,2048]{1,0:T(8,128)(2,1)}, bf16[128,2048]{1,0:T(8,128)(2,1)}, bf16[128,2048]{1,0:T(8,128)(2,1)}, bf16[8,96,256]{2,1,0:T(8,128)(2,1)}) custom-call(s32[1,4]{1,0:T(1,128)} %counts.1, s32[1,16]{1,0:T(1,128)} %slots.1, bf16[128,3072]{1,0:T(8,128)(2,1)} %g_in.1, bf16[128,2048]{1,0:T(8,128)(2,1)} %q_in.1, bf16[128,2048]{1,0:T(8,128)(2,1)} %k_in.1, ...), custom_call_target="tpu_custom_call" | custom-call | tf_op jit(solution)/shard_map/group_backward/pallas_call | solution.py:630
  140.4 2.6 %results.1 = (bf16[128,2048]{1,0:T(8,128)(2,1)}, bf16[128,2048]{1,0:T(8,128)(2,1)}, bf16[128,2048]{1,0:T(8,128)(2,1)}, f32[96,2048]{1,0:T(8,128)}) custom-call(bf16[128,2048]{1,0:T(8,128)(2,1)} %get-tuple-element.8.dq_in, bf16[128,2048]{1,0:T(8,128)(2,1)} %get-tuple-element.9.dk_in, bf16[128,2048]{1,0:T(8,128)(2,1)} %get-tuple-element.10.dv_in, ...), custom_call_target="tpu_custom_call" | custom-call | tf_op jit(solution)/shard_map/results/pallas_call | solution.py:692

commit v6 on v5

--- a/solution.py
+++ b/solution.py
@@ -109,6 +109,9 @@
     def cols(index):
         return pl.ds(pl.multiple_of(index * width, width), width)
 
+    def head_cols(index, i):
+        return pl.ds(pl.multiple_of(index * width + i * HEAD_DIM, HEAD_DIM), HEAD_DIM)
+
     def half_piece(index):
         return pl.ds(pl.multiple_of(index * piece, piece), piece)
 
@@ -355,6 +358,31 @@
     g_local().wait()
     arrived(g_chip.at[block(1 - core), :], g_sem.at[1])
 
+    for half in range(2):
+        axis = gather_axes[half][1]
+        for z in range(2):
+            w_two_wait(half, z, other(axis, 1 + (side - 2) * z))
+            for step in range(2, side - 1):
+                w_two_wait(half, z, other(axis, step))
+    def go_copy(c):
+        return remote(
+            go_send.at[c], go_all.at[chip_block(chip), :], go_send_sem.at[c], go_recv_sem.at[chip], cam=c * 2 + core
+        )
+
+    @pl.loop(0, CHIPS)
+    def _(u):
+        c = (chip + nth(u, 2, 1, 3, 0)) % CHIPS
+        grad_att = dot(g_chip[...], w_all[c].reshape(model, width), (1, 0)).astype(BF16)
+
+        @pl.when(u < CHIPS - 1)
+        def _():
+            go_send[c] = grad_att
+            go_copy(c).start()
+
+        @pl.when(u == CHIPS - 1)
+        def _():
+            go_all[chip_block(chip), :] = grad_att
+
     for step in range(1, CHIPS):
         c = (chip + step) % CHIPS
         arrived(att_recv.at[:, cols(c)], att_recv_sem.at[c])
@@ -403,95 +431,72 @@
             far_copy(half, part).start()
 
     for half in range(2):
-        axis = gather_axes[half][1]
-        for z in range(2):
-            w_two_wait(half, z, other(axis, 1 + (side - 2) * z))
-            for step in range(2, side - 1):
-                w_two_wait(half, z, other(axis, step))
-    def go_copy(c):
-        return remote(
-            go_send.at[c], go_all.at[chip_block(chip), :], go_send_sem.at[c], go_recv_sem.at[chip], cam=c * 2 + core
-        )
-
-    @pl.loop(0, CHIPS)
-    def _(u):
-        c = (chip + nth(u, 2, 1, 3, 0)) % CHIPS
-        grad_att = dot(g_chip[...], w_all[c].reshape(model, width), (1, 0)).astype(BF16)
-
-        @pl.when(u < CHIPS - 1)
-        def _():
-            go_send[c] = grad_att
-            go_copy(c).start()
-
-        @pl.when(u == CHIPS - 1)
-        def _():
-            go_all[chip_block(chip), :] = grad_att
-
-    for half in range(2):
         for part in range(2):
             first_copy(half, 1 - part, part).start()
 
-    def d_copy(j, target):
-        return remote(
-            d_send.at[j, block(target), :],
-            outs[j].at[:, cols(cam)],
-            d_send_sem.at[target, j],
-            d_recv_sem.at[cam, j],
+    def d_copy(j, i, target):
+        return remote(
+            d_send.at[j, block(target), i * HEAD_DIM : (i + 1) * HEAD_DIM],
+            outs[j].at[:, head_cols(cam, i)],
+            d_send_sem.at[target, j, i],
+            d_recv_sem.at[cam, j, i],
             cam=target,
         )
 
-    def d_local(j):
+    def d_local(j, i):
         return pltpu.make_async_copy(
-            d_send.at[j, block(cam), :], outs[j].at[:, cols(cam)], d_recv_sem.at[cam, j]
-        )
-
-    @pl.loop(0, CHIPS)
-    def _(t):
-        c = (chip + nth(t, 0, 3, 1, 2)) % CHIPS
+            d_send.at[j, block(cam), i * HEAD_DIM : (i + 1) * HEAD_DIM],
+            outs[j].at[:, head_cols(cam, i)],
+            d_recv_sem.at[cam, j, i],
+        )
+
+    def backward(c, i):
         here = chip_block(c)
-
-        @pl.when(t > 0)
-        def _():
-            arrived(go_all.at[here, :], go_recv_sem.at[c])
-
-        @pl.when(t == 2)
-        def _():
-            for half in range(2):
-                for part in range(2):
-                    arrived(far_recv.at[half, part], far_recv_sem.at[half, part])
-                    own = first_part(half, part, toward(half, part))
-                    own[...] = (own[...].astype(F32) + far_recv[half, part].astype(F32)).astype(BF16)
-                    first_copy(half, part, part).start()
-
-        for i in range(HEADS_HERE):
-            head = slice(i * HEAD_DIM, (i + 1) * HEAD_DIM)
-            go = go_all[here, head]
-            p = probs[i, here, :]
-            delta = jnp.sum(go.astype(F32) * att[here, head], axis=1, keepdims=True)
-            ds = (p * (dot(go, qkv[2, :, head], (1, 1)) - delta)).astype(BF16)
-            d_send[0, here, head] = (dot(ds, qkv[1, :, head], (1, 0)) * scale).astype(BF16)
-            dk_acc[:, head] += dot(ds, qkv[0, here, head], (0, 0))
-            dv_acc[:, head] += dot(p.astype(BF16), go, (0, 0))
-
-        @pl.when(t == 0)
-        def _():
-            d_local(0).start()
-            d_copy(0, sibling).start()
-
-        @pl.when(t > 0)
-        def _():
-            d_copy(0, c * 2).start()
-            d_copy(0, c * 2 + 1).start()
-
-    d_send[1] = (dk_acc[...] * scale).astype(BF16)
-    d_send[2] = dv_acc[...].astype(BF16)
-    for j in range(1, 3):
-
-        @pl.loop(1, 8)
-        def _(step):
-            d_copy(j, (cam + step) % 8).start()
-
-        d_local(j).start()
+        head = slice(i * HEAD_DIM, (i + 1) * HEAD_DIM)
+        go = go_all[here, head]
+        p = probs[i, here, :]
+        delta = jnp.sum(go.astype(F32) * att[here, head], axis=1, keepdims=True)
+        ds = (p * (dot(go, qkv[2, :, head], (1, 1)) - delta)).astype(BF16)
+        d_send[0, here, head] = (dot(ds, qkv[1, :, head], (1, 0)) * scale).astype(BF16)
+        dk_acc[:, head] += dot(ds, qkv[0, here, head], (0, 0))
+        dv_acc[:, head] += dot(p.astype(BF16), go, (0, 0))
+
+    for i in range(HEADS_HERE):
+        backward(chip, i)
+        d_local(0, i).start()
+        d_copy(0, i, sibling).start()
+
+    for i in range(HEADS_HERE):
+        head = slice(i * HEAD_DIM, (i + 1) * HEAD_DIM)
+
+        @pl.loop(1, CHIPS)
+        def _(t):
+            c = (chip + nth(t, 0, 3, 1, 2)) % CHIPS
+            if i == 0:
+                arrived(go_all.at[chip_block(c), :], go_recv_sem.at[c])
+
+                @pl.when(t == 2)
+                def _():
+                    for half in range(2):
+                        for part in range(2):
+                            arrived(far_recv.at[half, part], far_recv_sem.at[half, part])
+                            own = first_part(half, part, toward(half, part))
+                            own[...] = (own[...].astype(F32) + far_recv[half, part].astype(F32)).astype(BF16)
+                            first_copy(half, part, part).start()
+
+            backward(c, i)
+            d_copy(0, i, c * 2).start()
+            d_copy(0, i, c * 2 + 1).start()
+
+        d_send[1, :, head] = (dk_acc[:, head] * scale).astype(BF16)
+        d_send[2, :, head] = dv_acc[:, head].astype(BF16)
+        for j in range(1, 3):
+
+            @pl.loop(1, 8)
+            def _(step):
+                d_copy(j, i, (cam + step) % 8).start()
+
+            d_local(j, i).start()
 
     def second_copy(half, step):
         axis = reduce_axes[half][1]
@@ -576,7 +581,8 @@
 
         @pl.loop(0, 8)
         def _(source):
-            arrived(outs[j].at[:, cols(source)], d_recv_sem.at[source, j])
+            for i in range(HEADS_HERE):
+                arrived(outs[j].at[:, head_cols(source, i)], d_recv_sem.at[source, j, i])
 
     arrived(land_out.at[cam], land_recv_sem.at[cam])
     for step in range(CHIPS):
@@ -607,7 +613,8 @@
     def _(step):
         for j in range(3):
             qkv_copy(j, step).wait_send()
-            d_copy(j, (cam + step) % 8).wait_send()
+            for i in range(HEADS_HERE):
+                d_copy(j, i, (cam + step) % 8).wait_send()
         line_copy(step).wait_send()
 
     for step in range(CHIPS):
@@ -671,8 +678,8 @@
             dma((CHIPS,)),
             dma((CHIPS,)),
             dma((CHIPS,)),
-            dma((8, 3)),
-            dma((8, 3)),
+            dma((8, 3, HEADS_HERE)),
+            dma((8, 3, HEADS_HERE)),
             dma((2, 2)),
             dma((2, 2)),
             dma((2, 2, 2)),

time: 143 us -> 142 us (level)
    pallas_call x1, Pallas kernels: 140 us -> 138 us  [local(): pl.pallas_call(functools.partial(kernel, dims), out_shape=(gradient, grad...]
where the time goes in v6:
time: 142 us; the launch traced here: 141 us
  Pallas kernels  141 us (99%)
    pallas_call x1, Pallas kernels, local(): pl.pallas_call(functools.partial(kernel, dims), out_shape=(gradient, grad...  138 us

profile of v6, /device:TPU:1, one launch (start us, length us, event | category | flops | bytes accessed | tf_op | source)
XLA Modules:
  0.0 141.4 jit_solution(9793060483594124781)
XLA Ops:
  0.6 138.2 %group_backward.1 = (bf16[128,2048]{1,0:T(8,128)(2,1)}, bf16[128,2048]{1,0:T(8,128)(2,1)}, bf16[128,2048]{1,0:T(8,128)(2,1)}, bf16[8,96,256]{2,1,0:T(8,128)(2,1)}) custom-call(s32[1,4]{1,0:T(1,128)} %counts.1, s32[1,16]{1,0:T(1,128)} %slots.1, bf16[128,3072]{1,0:T(8,128)(2,1)} %g_in.1, bf16[128,2048]{1,0:T(8,128)(2,1)} %q_in.1, bf16[128,2048]{1,0:T(8,128)(2,1)} %k_in.1, ...), custom_call_target="tpu_custom_call" | custom-call | tf_op jit(solution)/shard_map/group_backward/pallas_call | solution.py:637
  138.8 2.6 %results.1 = (bf16[128,2048]{1,0:T(8,128)(2,1)}, bf16[128,2048]{1,0:T(8,128)(2,1)}, bf16[128,2048]{1,0:T(8,128)(2,1)}, f32[96,2048]{1,0:T(8,128)}) custom-call(bf16[128,2048]{1,0:T(8,128)(2,1)} %get-tuple-element.8.dq_in, bf16[128,2048]{1,0:T(8,128)(2,1)} %get-tuple-element.9.dk_in, bf16[128,2048]{1,0:T(8,128)(2,1)} %get-tuple-element.10.dv_in, ...), custom_call_target="tpu_custom_call" | custom-call | tf_op jit(solution)/shard_map/results/pallas_call | solution.py:699

commit v7 on v6

--- a/solution.py
+++ b/solution.py
@@ -289,6 +289,11 @@
     dk_acc[...] = jnp.zeros_like(dk_acc)
     dv_acc[...] = jnp.zeros_like(dv_acc)
 
+    def qkv_wait(j):
+        @pl.loop(0, 8)
+        def _(source):
+            arrived(qkv.at[j, block(source), :], qkv_recv_sem.at[source, j])
+
     for z in (z_lo, 1 - z_lo):
         for half in range(2):
             axis = gather_axes[half][0]
@@ -297,13 +302,9 @@
                 arrived(w_one_ref(half, z, c), w_one_recv.at[half, z, c])
             for way in range(2):
                 w_two(half, z, way).start()
-        if z is z_lo:
-            qkv_start(2)
-    for j in range(3):
-
-        @pl.loop(0, 8)
-        def _(source):
-            arrived(qkv.at[j, block(source), :], qkv_recv_sem.at[source, j])
+    qkv_wait(0)
+    qkv_start(2)
+    qkv_wait(1)
 
     def att_copy(c):
         return remote(
@@ -335,9 +336,25 @@
                 exps = jnp.exp(scores - jnp.max(scores, axis=1, keepdims=True))
                 p = exps * (1.0 / jnp.sum(exps, axis=1, keepdims=True))
                 probs[i, here, :] = p
-                att[here, head] = dot(p.astype(BF16), qkv[2, :, head], (1, 0))
-
+
+    qkv_wait(2)
+
+    @pl.loop(0, CHIPS)
+    def _(u):
+        c = (chip + nth(u, 2, 1, 3, 0)) % CHIPS
         there = chip_block(c)
+        for i in range(HEADS_HERE):
+            head = slice(i * HEAD_DIM, (i + 1) * HEAD_DIM)
+            att[there, head] = dot(probs[i, there, :].astype(BF16), qkv[2, :, head], (1, 0))
+
+        @pl.when(u < CHIPS - 1)
+        def _():
+            att_send[there, :] = att[there, :].astype(BF16)
+            att_copy(c).start()
+
+        @pl.when(u == CHIPS - 1)
+        def _():
+            att_recv[:, cols(chip)] = att[there, :].astype(BF16)
 
         @pl.when(u < 2)
         def _():
@@ -345,15 +362,6 @@
             for half in range(2):
                 w_two_wait(half, z, w_from(half, z))
                 w_pass(half, z).start()
-
-        @pl.when(u < CHIPS - 1)
-        def _():
-            att_send[there, :] = att[there, :].astype(BF16)
-            att_copy(c).start()
-
-        @pl.when(u == CHIPS - 1)
-        def _():
-            att_recv[:, cols(chip)] = att[there, :].astype(BF16)
 
     g_local().wait()
     arrived(g_chip.at[block(1 - core), :], g_sem.at[1])

time: 142 us -> 140 us (0.986)
  Pallas kernels: 141 us -> 139 us
    pallas_call x1, Pallas kernels: 138 us -> 136 us  [local(): pl.pallas_call(functools.partial(kernel, dims), out_shape=(gradient, grad...]
where the time goes in v7:
time: 140 us
  Pallas kernels  139 us (99%)
    pallas_call x1, Pallas kernels, local(): pl.pallas_call(functools.partial(kernel, dims), out_shape=(gradient, grad...  136 us

profile of v7, /device:TPU:1, one launch (start us, length us, event | category | flops | bytes accessed | tf_op | source)
XLA Modules:
  0.0 139.6 jit_solution(10819937490762777949)
XLA Ops:
  0.6 136.3 %group_backward.1 = (bf16[128,2048]{1,0:T(8,128)(2,1)}, bf16[128,2048]{1,0:T(8,128)(2,1)}, bf16[128,2048]{1,0:T(8,128)(2,1)}, bf16[8,96,256]{2,1,0:T(8,128)(2,1)}) custom-call(s32[1,4]{1,0:T(1,128)} %counts.1, s32[1,16]{1,0:T(1,128)} %slots.1, bf16[128,3072]{1,0:T(8,128)(2,1)} %g_in.1, bf16[128,2048]{1,0:T(8,128)(2,1)} %q_in.1, bf16[128,2048]{1,0:T(8,128)(2,1)} %k_in.1, ...), custom_call_target="tpu_custom_call" | custom-call | tf_op jit(solution)/shard_map/group_backward/pallas_call | solution.py:645
  137.0 2.6 %results.1 = (bf16[128,2048]{1,0:T(8,128)(2,1)}, bf16[128,2048]{1,0:T(8,128)(2,1)}, bf16[128,2048]{1,0:T(8,128)(2,1)}, f32[96,2048]{1,0:T(8,128)}) custom-call(bf16[128,2048]{1,0:T(8,128)(2,1)} %get-tuple-element.8.dq_in, bf16[128,2048]{1,0:T(8,128)(2,1)} %get-tuple-element.9.dk_in, bf16[128,2048]{1,0:T(8,128)(2,1)} %get-tuple-element.10.dv_in, ...), custom_call_target="tpu_custom_call" | custom-call | tf_op jit(solution)/shard_map/results/pallas_call | solution.py:707
